TPU v7x, 256 devices: a whole 4x4x8 slice. The times are simulated.
256 devices in a mesh: dp: 64 (over z, y, core), mp: 4 (over x).
Axes of the slice: x: 4, y: 4, z: 8, core: 2. Of those that a mesh axis runs over, the one named last changes fastest.
Arguments:
- weights: bfloat16 [14336, 8, 128], P('mp'), may hold values from -0.1875 to 0.1875
- hidden: bfloat16 [16384, 14336], P('dp', 'mp'), may hold values from -6 to 6
- cotangent: bfloat16 [16384, 8192], P('dp', 'mp'), may hold values from -6 to 6
- sketch: float32 [128, 8192], P(None, ('dp', 'mp')), may hold values from -0.046875 to 0.046875
- projection: float32 [128, 4, 3584], P(None, 'mp', 'dp'), may hold values from -0.046875 to 0.046875
- pattern: int32 [112, 8], P('mp'), may hold values from 0 to 63, as said below
Outputs:
- input_grad: bfloat16 [16384, 14336], P('dp', 'mp')
- direction: float32 [4, 3584, 8, 128], P('mp', 'dp')
Inputs may be any that keep to these rules, and one draw needn't show every extreme that they name: `pattern`: each block row names 8 different column blocks.
All inputs are finite; a program needn't handle non-finite values.
Results may differ from a plain program's by a relative error of at most 0.001.
Values may be sent and summed in bfloat16 or wider, within the bound.
A program may use at most 192 MiB of HBM per device.

v0:
```python
import math

import jax
import jax.numpy as jnp
from jax import lax
from jax.sharding import PartitionSpec as P

NS_STEPS = 5


shift_eps = 0.0001


def matmul(operand_a, operand_b):
    return jnp.dot(
        operand_a, operand_b, precision=lax.Precision.HIGHEST, preferred_element_type=jnp.float32
    )


def root_factor(gram):
    identity = jnp.eye(gram.shape[0], dtype=jnp.float32)
    shifted = gram + shift_eps * identity
    frobenius = jnp.sqrt(jnp.sum(shifted * shifted))
    root_iter = shifted / frobenius
    inverse_iter = identity
    for iteration in range(NS_STEPS):
        middle = 0.5 * (3.0 * identity - matmul(inverse_iter, root_iter))
        root_iter = matmul(root_iter, middle)
        inverse_iter = matmul(middle, inverse_iter)
    shifted_root = (
        0.5 * jnp.sqrt(frobenius) * (root_iter + root_iter.T) + math.sqrt(shift_eps) * identity
    )
    factor = jnp.linalg.cholesky(shifted_root)
    solved = jax.scipy.linalg.cho_solve((factor, True), inverse_iter.T)
    return -solved.T / (math.sqrt(shift_eps) * jnp.sqrt(frobenius))


def per_device(weights, hidden, cotangent, sketch, projection, pattern):
    highest = lax.Precision.HIGHEST
    tok_rows = hidden.shape[0]
    mp_rows = weights.shape[0]
    slots = weights.shape[1]
    block_size = weights.shape[2]
    block_rows = mp_rows // block_size
    dp_size = lax.axis_size("dp")
    dev_rows = mp_rows // dp_size
    all_tokens = tok_rows * dp_size
    rank = sketch.shape[0]
    full_cot = lax.all_gather(cotangent, "mp", axis=1, tiled=True)
    width = full_cot.shape[1]
    col_blocks = width // block_size
    cot_blocks = full_cot.reshape(tok_rows, col_blocks, block_size)
    chosen = jnp.take(cot_blocks, pattern.reshape(-1), axis=1).reshape(
        tok_rows, block_rows, slots, block_size
    )
    weight_blocks = weights.reshape(block_rows, block_size, slots, block_size)
    input_grad = jnp.einsum(
        "trkn,rikn->tri", chosen, weight_blocks, preferred_element_type=jnp.float32
    )
    input_grad = input_grad.reshape(tok_rows, mp_rows).astype(jnp.bfloat16)
    hidden_blocks = hidden.reshape(tok_rows, block_rows, block_size)
    local_grad = (
        jnp.einsum("tri,trkn->rikn", hidden_blocks, chosen, preferred_element_type=jnp.float32)
        / all_tokens
    )
    local_grad = local_grad.reshape(mp_rows, slots, block_size)
    grad_rows = lax.psum_scatter(local_grad, "dp", scatter_dimension=0, tiled=True)
    group_count = (dev_rows - 1) // block_size + 2
    row_start = lax.axis_index("dp") * dev_rows
    row_block = (row_start + jnp.arange(dev_rows, dtype=jnp.int32)) // block_size
    first_block = row_start // block_size
    group_blocks = first_block + jnp.arange(group_count, dtype=jnp.int32)
    member = (row_block[:, None] == group_blocks[None, :]).astype(jnp.float32)
    group_cols = jnp.take(pattern, jnp.minimum(group_blocks, block_rows - 1), axis=0)
    proj_rows = projection.reshape(rank, dev_rows)
    masked_proj = proj_rows[:, :, None] * member[None, :, :]
    per_group = jnp.einsum("mib,ikn->mbkn", masked_proj, grad_rows, precision=highest)
    start = jnp.zeros((rank, col_blocks, block_size), jnp.float32)
    compress_part = start.at[:, group_cols, :].add(per_group)
    compress_part = compress_part.reshape(rank, width)
    compressed = lax.psum(compress_part, ("dp", "mp"))
    sketch_full = lax.all_gather(sketch, ("dp", "mp"), axis=1, tiled=True)
    stacked = jnp.concatenate([sketch_full, compressed], axis=0)
    gram = matmul(stacked, stacked.T)
    mixing = root_factor(gram)
    stacked_blocks = stacked.reshape(2 * rank, col_blocks, block_size)
    selected = jnp.take(stacked_blocks, group_cols, axis=1)
    projected_all = jnp.einsum("ikn,mbkn->ibm", grad_rows, selected, precision=highest)
    projected = jnp.einsum("ibm,ib->im", projected_all, member, precision=highest)
    mixed = matmul(projected, mixing)
    corr_all = jnp.einsum("im,mbkn->ibkn", mixed, selected, precision=highest)
    correction = jnp.einsum("ibkn,ib->ikn", corr_all, member, precision=highest)
    direction = grad_rows / math.sqrt(shift_eps) + correction
    return (input_grad, direction.reshape(1, dev_rows, slots, block_size))


def solution(mesh):
    return jax.shard_map(
        per_device,
        mesh=mesh,
        in_specs=(
            P("mp", None, None),
            P("dp", "mp"),
            P("dp", "mp"),
            P(None, ("dp", "mp")),
            P(None, "mp", "dp"),
            P("mp", None),
        ),
        out_specs=(P("dp", "mp"), P("mp", "dp", None, None)),
        check_vma=False,
    )
```

profile of v0, /device:TPU:1, one launch (start us, length us, event | category | flops | bytes accessed | tf_op | source)
XLA Modules:
  0.0 681.7 jit_solution(7993357652619971913)
XLA Ops:
  8.0 2.3 copy.27
  12.0 2.9 copy.31
  15.0 50.9 %all-gather.3.cloned.1.call-done = bf16[256,8192]{0,1:T(8,128)(2,1)} async-done(((bf16[256,2048]{0,1:T(8,128)(2,1)}), bf16[256,8192]{0,1:T(8,128)(2,1)}) %all-gather.3.cloned.1.call-update) | async-done | bytes 4194320 | tf_op jit(solution)/shard_map/all_gather | solution.py:49
  65.8 6.4 copy.29
  72.2 11.4 %gather_fusion = bf16[224,256,128]{2,1,0:T(8,128)(2,1)} fusion(bf16[256,64,128]{2,0,1:T(8,128)(2,1)} %copy.29, s32[1024]{0:T(1024)S(1)} %pad_clamp_fusion.2), kind=kCustom, calls=%fused_computation | custom fusion | bytes 29361024 | tf_op jit(solution)/shard_map/jit(_take)/gather | solution.py:53
  83.7 10.4 %multiply_bitcast_fusion = f32[28,128,8,128]{3,1,2,0:T(8,128)} fusion(bf16[256,28,128,1]{0,2,3,1:T(8,128)(2,1)S(1)} %bitcast.150, bf16[256,28,8,128]{3,0,2,1:T(8,128)(2,1)} %bitcast.143, pred[28,8]{1,0:T(8,128)(4,1)S(1)} %copy.26), kind=kOutput, calls=%fused_computation.6 | convolution fusion | flops 1890058240 | bytes 31195360 | tf_op jit(solution)/shard_map/tri,trkn->rikn/dot_general | solution.py:63
  94.1 23.7 %copy.32 = f32[28,128,8,128]{3,2,1,0:T(8,128)} copy(f32[28,128,8,128]{3,1,2,0:T(8,128)} %multiply_bitcast_fusion) | data formatting | bytes 29360128 | tf_op jit(solution)/shard_map/div | solution.py:63
  119.7 165.1 %reduce-scatter.2.cloned.1.call-done = f32[56,8,128]{2,1,0:T(8,128)} async-done(((f32[3584,8,128]{2,1,0:T(8,128)}), f32[56,8,128]{2,1,0:T(8,128)}) %reduce-scatter.2.cloned.1.call-update) | async-done | bytes 229392 | tf_op jit(solution)/shard_map/reduce_scatter | solution.py:67
  286.8 2.5 broadcast_in_dim.41
  289.3 3.4 scatter_fusion
  292.7 5.6 copy.35
  298.3 9.9 %bitcast_convert_fusion = bf16[28,256,128]{1,2,0:T(8,128)(2,1)S(1)} fusion(bf16[28,128,8,128]{3,2,1,0:T(8,128)(2,1)} %bitcast.157, bf16[256,28,8,128]{3,0,2,1:T(8,128)(2,1)} %bitcast.144, pred[28,8]{1,0:T(8,128)(4,1)S(1)} %copy.26), kind=kOutput, calls=%fused_computation.13 | convolution fusion | flops 1887305728 | bytes 23855328 | tf_op jit(solution)/shard_map/trkn,rikn->tri/dot_general | solution.py:57
  308.3 2.6 copy.39
  310.8 4.6 constant_dynamic-update-slice_fusion.1
  315.4 251.8 %all-reduce.3.cloned.1.call-done = f32[128,8192]{0,1:T(8,128)} async-done(((f32[128,8192]{0,1:T(8,128)}), f32[128,8192]{0,1:T(8,128)}) %all-reduce.3.cloned.1.call-update) | async-done | bytes 4194320 | tf_op jit(solution)/shard_map/psum | solution.py:81
  567.2 4.5 constant_dynamic-update-slice_fusion
  571.7 20.0 %multiply_reduce_fusion = (f32[]{:T(128)}, f32[256,256]{1,0:T(8,128)S(1)}) fusion(f32[256,8192]{0,1:T(8,128)} %constant_dynamic-update-slice_fusion), kind=kOutput, calls=%fused_computation.51 | convolution fusion | flops 6442778624 | bytes 8650756 | tf_op jit(solution)/shard_map/dot_general | solution.py:15
  597.9 11.7 %cholesky.49 = f32[128,128]{1,0:T(8,128)S(1)} custom-call(f32[128,128]{1,0:T(8,128)S(1)} %cholesky.115), custom_call_target="Cholesky" | custom-call | tf_op jit(solution)/shard_map/jit(cholesky)/cholesky | solution.py:33
  610.3 5.5 gather_fusion.2
  617.8 9.8 %custom-call.18 = f32[1,128,128]{1,2,0:T(8,128)S(1)} custom-call(f32[1,128,128]{2,1,0:T(8,128)S(1)} %get-tuple-element.29), custom_call_target="InvertDiagBlocksLowerTriangular" | custom-call | tf_op jit(solution)/shard_map/jit(cholesky)/cholesky | solution.py:33
  628.1 11.7 %cholesky.103 = f32[128,128]{1,0:T(8,128)S(1)} custom-call(f32[128,128]{1,0:T(8,128)S(1)} %convolution_subtract_fusion.7), custom_call_target="Cholesky" | custom-call | tf_op jit(solution)/shard_map/jit(cholesky)/cholesky | solution.py:33
  642.0 4.1 while.1
  646.0 19.9 %custom-call.19 = f32[2,128,128]{1,2,0:T(8,128)S(1)} custom-call(f32[2,128,128]{2,1,0:T(8,128)S(1)} %get-tuple-element.9), custom_call_target="InvertDiagBlocksLowerTriangular" | custom-call | tf_op jit(solution)/shard_map/jit(_cho_solve)/triangular_solve | solution.py:34
  667.7 2.3 fusion.18
  (79 shorter events, 24.9 us)
Async XLA Ops:
  8.0 57.8 %all-gather.3.cloned.1.call-start = ((), (), s32[]{:S(2)}) async-start(), calls=%async_computation.1 | async-start | bytes 5242880 | tf_op jit(solution)/shard_map/all_gather | solution.py:49
  10.3 274.4 %reduce-scatter.2.cloned.1.call-start = ((), (), s32[]{:S(2)}) async-start(), calls=%async_computation.2 | async-start | bytes 14909440 | tf_op jit(solution)/shard_map/reduce_scatter | solution.py:67
  117.8 167.0 %copy-start.1 = (f32[128,1,56]{0,2,1:T(8,128)S(1)}, f32[128,1,56]{0,2,1:T(8,128)}, u32[]{:S(2)}) copy-start(f32[128,1,56]{0,2,1:T(8,128)} %param.10) | copy-start | bytes 86020
  117.8 193.0 %all-gather.5.cloned.1.call-start = ((), (), s32[]{:S(2)}) async-start(), calls=%async_computation.3 | async-start | bytes 4210688 | tf_op jit(solution)/shard_map/all_gather | solution.py:82
  118.4 448.9 %all-reduce.3.cloned.1.call-start = ((), (), s32[]{:S(2)}) async-start(), calls=%async_computation.4 | async-start | bytes 8388608 | tf_op jit(solution)/shard_map/psum | solution.py:81
  597.8 69.9 %copy-start = (f32[56,8,128]{2,1,0:T(8,128)S(1)}, f32[56,8,128]{2,1,0:T(8,128)}, u32[]{:S(2)}) copy-start(f32[56,8,128]{2,1,0:T(8,128)} %reduce-scatter.2.cloned.1.call-done) | copy-start | bytes 688132
Sparse Core Ops, SparseCore 0:
  11.2 54.5 all-gather.2
  117.9 166.8 reduce-scatter.1
Sparse Core Ops, SparseCore 1:
  122.0 130.9 all-gather.4
  298.4 268.8 all-reduce.2
where the time goes:
time: 687 us; the launch traced here: 682 us
  waiting for transfers between devices  468 us (68%)
  local copies, waits for them, and re-layouts  80.1 us (12%)
  other arithmetic  59.1 us (9%)
  matrix products  55.9 us (8%)
  between operations  18.1 us (3%)
    psum x1, waiting for transfers between devices, per_device(): compressed = lax.psum(compress_part, ('dp', 'mp'))  252 us
    reduce_scatter x1, waiting for transfers between devices, per_device(): lax.psum_scatter(local_grad, 'dp', scatter_dimension=0, tiled=True)  165 us
    all_gather x1, waiting for transfers between devices, per_device(): full_cot = lax.all_gather(cotangent, 'mp', axis=1, tiled=True)  50.9 us
    another operation x6, other arithmetic, root_factor(): factor = jnp.linalg.cholesky(shifted_root)  34 us
    dot_general x17, matrix products, matmul(): jnp.dot(operand_a, operand_b, precision=lax.Precision.HIGHEST, preferred_...  26.2 us
    div x1, local copies, waits for them, and re-layouts, per_device(): jnp.einsum('tri,trkn->rikn', hidden_blocks, chosen, preferred_element_typ...  23.7 us
    another operation x3, other arithmetic, root_factor(): solved = jax.scipy.linalg.cho_solve((factor, True), inverse_iter.T)  19.9 us
  transfers between devices with their start and end apart: 4, of which 3 were waited for; matrix products, arithmetic and copies ran while one was open for 5% of the time, Pallas kernels for 0%

commit v1 on v0

v1 whole, which is shorter than its diff:
```python
import functools
import math

import jax
import jax.numpy as jnp
from jax import lax
from jax.experimental import pallas as pl
from jax.experimental.pallas import tpu as pltpu
from jax.sharding import PartitionSpec as P

NS_STEPS = 5
EPS = 0.0001
F32 = jnp.float32
BF16 = jnp.bfloat16
MIB = 1 << 20


def split_bf16(value):
    high = value.astype(BF16)
    low = (value - high.astype(F32)).astype(BF16)
    return high, low


def exact_dot(left, right, dims):
    return lax.dot_general(
        left, right, (dims, ((), ())), precision=lax.Precision.HIGHEST, preferred_element_type=F32
    )


def local_kernel(inv_tokens, pat_ref, cot_ref, hid_ref, wgt_ref, proj_ref, back_ref, grad_ref, comp_ref, z_ref):
    step = pl.program_id(0)
    slots = wgt_ref.shape[0]
    blk = hid_ref.shape[1]
    per_part = cot_ref.shape[2] // blk
    col_blocks = cot_ref.shape[0] * per_part

    def cot_block(col):
        lane = pl.multiple_of(lax.rem(col, per_part) * blk, blk)
        return cot_ref[lax.div(col, per_part), :, pl.ds(lane, blk)]

    @pl.when(step == 0)
    def _():
        @pl.loop(0, col_blocks)
        def _(col):
            z_ref[col] = jnp.zeros(z_ref.shape[1:], F32)

    cols = [pat_ref[step, k] for k in range(slots)]
    chosen = jnp.concatenate([cot_block(col) for col in cols], axis=1)
    weight = jnp.concatenate([wgt_ref[k] for k in range(slots)], axis=1)
    back = lax.dot_general(chosen, weight, (((1,), (1,)), ((), ())), preferred_element_type=F32)
    back_ref[...] = back.astype(BF16)
    hid = hid_ref[...]
    grad = lax.dot_general(hid, chosen, (((0,), (0,)), ((), ())), preferred_element_type=F32)
    grad = grad * inv_tokens
    for k in range(slots):
        grad_ref[k] = grad[:, k * blk : (k + 1) * blk]
    high, low = split_bf16(proj_ref[...])
    both = jnp.dot(hid, jnp.concatenate([high, low], axis=1), preferred_element_type=F32)
    rank = proj_ref.shape[1]
    y = both[:, :rank] + both[:, rank:]
    for col in cols:
        z_ref[col] += y

    @pl.when(step == pl.num_programs(0) - 1)
    def _():
        @pl.loop(0, col_blocks)
        def _(col):
            zh, zl = split_bf16(z_ref[col])
            out = lax.dot_general(
                cot_block(col),
                jnp.concatenate([zh, zl], axis=1),
                (((0,), (0,)), ((), ())),
                preferred_element_type=F32,
            )
            comp_ref[col] = (out[:, :rank] + out[:, rank:]) * inv_tokens


def local_step(pattern, cot, hidden, weights, proj, all_tokens):
    parts, tokens, part_cols = cot.shape
    block_rows, slots = pattern.shape
    blk = weights.shape[2]
    rows = hidden.shape[1]
    rank = proj.shape[1]
    col_blocks = parts * part_cols // blk
    grid_spec = pltpu.PrefetchScalarGridSpec(
        num_scalar_prefetch=1,
        grid=(block_rows,),
        in_specs=[
            pl.BlockSpec((parts, tokens, part_cols), lambda r, pat: (0, 0, 0), pipeline_mode=pl.Buffered(1)),
            pl.BlockSpec((tokens, blk), lambda r, pat: (0, r)),
            pl.BlockSpec((slots, blk, blk), lambda r, pat: (0, r, 0)),
            pl.BlockSpec((blk, rank), lambda r, pat: (r, 0)),
        ],
        out_specs=[
            pl.BlockSpec((tokens, blk), lambda r, pat: (0, r)),
            pl.BlockSpec((slots, blk, blk), lambda r, pat: (0, r, 0)),
            pl.BlockSpec((col_blocks, blk, rank), lambda r, pat: (0, 0, 0), pipeline_mode=pl.Buffered(1)),
        ],
        scratch_shapes=[pltpu.VMEM((col_blocks, tokens, rank), F32)],
    )
    return pl.pallas_call(
        functools.partial(local_kernel, 1.0 / all_tokens),
        grid_spec=grid_spec,
        out_shape=(
            jax.ShapeDtypeStruct((tokens, rows), BF16),
            jax.ShapeDtypeStruct((slots, rows, blk), F32),
            jax.ShapeDtypeStruct((col_blocks, blk, rank), F32),
        ),
        compiler_params=pltpu.CompilerParams(vmem_limit_bytes=48 * MIB),
        cost_estimate=pl.CostEstimate(flops=6_000_000_000, bytes_accessed=36_000_000, transcendentals=0),
        name="local_step",
    )(pattern, cot, hidden, weights, proj)


def identity(n):
    rows = lax.broadcasted_iota(jnp.int32, (n, n), 0)
    cols = lax.broadcasted_iota(jnp.int32, (n, n), 1)
    return jnp.where(rows == cols, 1.0, 0.0).astype(F32)


def mul(left, right):
    return exact_dot(left, right, ((1,), (0,)))


def spd_inverse(mat, eye):
    n = mat.shape[0]
    bound = jnp.max(jnp.sum(jnp.abs(mat), axis=1, keepdims=True))
    start = eye * (2.0 / (bound + math.sqrt(EPS)))

    def unfinished(state):
        count, previous, residual, _ = state
        return (count < 100) & (residual > 2e-6) & ((residual < 0.5 * previous) | (residual > 0.1))

    def body(state):
        count, _, residual, guess = state
        gap = eye - mul(mat, guess)
        guess = guess + mul(guess, gap)
        return count + 1, residual, jnp.max(jnp.abs(gap)), guess

    state = lax.while_loop(unfinished, body, (0, jnp.float32(4.0), jnp.float32(2.0), start))
    return state[3]


def mixing_of(gram):
    n = gram.shape[0]
    eye = identity(n)
    shifted = gram + EPS * eye
    total = jnp.sum(jnp.sum(shifted * shifted, axis=1, keepdims=True), axis=0, keepdims=True)
    frob = jnp.sqrt(total)
    root = shifted / frob
    middle = 1.5 * eye - 0.5 * root
    root = mul(root, middle)
    inverse = middle
    for _ in range(NS_STEPS - 1):
        middle = 1.5 * eye - 0.5 * mul(inverse, root)
        root = mul(root, middle)
        inverse = mul(middle, inverse)
    half = 0.5 * jnp.sqrt(frob) * (root + root.T) + math.sqrt(EPS) * eye
    half_inv = spd_inverse(half, eye)
    return -mul(inverse, half_inv) / (math.sqrt(EPS) * jnp.sqrt(frob))


def finish_kernel(row_ref, pat_ref, grad_ref, sketch_ref, comp_ref, out_ref, gram_ref, sel_ref):
    slots, rows, blk = grad_ref.shape
    rank = comp_ref.shape[1]
    width = comp_ref.shape[0]
    chunk = 1024
    gram_ref[...] = jnp.zeros_like(gram_ref)

    @pl.loop(0, width // chunk)
    def _(i):
        at = pl.ds(pl.multiple_of(i * chunk, chunk), chunk)
        st = jnp.concatenate([sketch_ref[at, :], comp_ref[at, :]], axis=1)
        high, low = split_bf16(st)
        dims = (((0,), (0,)), ((), ()))
        gram_ref[0] += lax.dot_general(high, high, dims, preferred_element_type=F32)
        gram_ref[1] += lax.dot_general(high, low, dims, preferred_element_type=F32)

    cross = gram_ref[1]
    mixing = mixing_of(gram_ref[0] + (cross + cross.T))
    start = row_ref[0]
    first = lax.div(start, blk)
    last = pat_ref.shape[0] - 1
    grad = jnp.concatenate([grad_ref[k] for k in range(slots)], axis=1)
    block_of = lax.div(start + lax.broadcasted_iota(jnp.int32, (rows, 1), 0), blk)
    projected = None
    for g in range(2):
        brow = jnp.minimum(first + g, last)
        for k in range(slots):
            col = pl.multiple_of(pat_ref[brow, k] * blk, blk)
            here = pl.ds(k * blk, blk)
            sel_ref[g, here, :rank] = sketch_ref[pl.ds(col, blk), :]
            sel_ref[g, here, rank:] = comp_ref[pl.ds(col, blk), :]
        part = mul(grad, sel_ref[g])
        projected = part if projected is None else jnp.where(block_of == first + g, part, projected)
    mixed = mul(projected, mixing)
    corr = exact_dot(mixed, sel_ref[0], ((1,), (1,)))
    corr1 = exact_dot(mixed, sel_ref[1], ((1,), (1,)))
    corr = jnp.where(block_of == first + 1, corr1, corr)
    result = grad * (1.0 / math.sqrt(EPS)) + corr
    for k in range(slots):
        out_ref[:, k, :] = result[:, k * blk : (k + 1) * blk]


def finish(start_row, pattern, grad, sketch_t, comp_t):
    slots, rows, blk = grad.shape
    rank = comp_t.shape[1]
    smem = pl.BlockSpec(memory_space=pltpu.SMEM)
    vmem = pl.BlockSpec(memory_space=pltpu.VMEM)
    return pl.pallas_call(
        finish_kernel,
        in_specs=[smem, smem, vmem, vmem, vmem],
        out_specs=vmem,
        out_shape=jax.ShapeDtypeStruct((rows, slots, blk), F32),
        scratch_shapes=[
            pltpu.VMEM((2, 2 * rank, 2 * rank), F32),
            pltpu.VMEM((2, slots * blk, 2 * rank), F32),
        ],
        compiler_params=pltpu.CompilerParams(vmem_limit_bytes=40 * MIB),
        cost_estimate=pl.CostEstimate(flops=5_000_000_000, bytes_accessed=9_000_000, transcendentals=0),
        name="finish",
    )(start_row, pattern, grad, sketch_t, comp_t)


def per_device(weights, hidden, cotangent, sketch, projection, pattern):
    rank = sketch.shape[0]
    slots, blk = weights.shape[1:]
    dp_size = lax.axis_size("dp")
    dev_rows = weights.shape[0] // dp_size
    all_tokens = hidden.shape[0] * dp_size
    cot = lax.all_gather(cotangent, "mp")
    proj = lax.all_gather(projection.reshape(rank, dev_rows).T, "dp", tiled=True)
    sketch_t = lax.all_gather(sketch.T, ("dp", "mp"), tiled=True)
    weights_t = weights.transpose(1, 0, 2)
    input_grad, grad, comp = local_step(pattern, cot, hidden, weights_t, proj, all_tokens)
    comp = comp.reshape(-1, rank)
    comp_piece = lax.psum_scatter(comp, ("dp", "mp"), scatter_dimension=0, tiled=True)
    comp_t = lax.all_gather(comp_piece, ("dp", "mp"), tiled=True)
    grad = lax.psum_scatter(grad, "dp", scatter_dimension=1, tiled=True)
    start_row = (lax.axis_index("dp") * dev_rows).reshape(1).astype(jnp.int32)
    direction = finish(start_row, pattern, grad, sketch_t, comp_t)
    return input_grad, direction[None]


def solution(mesh):
    return jax.shard_map(
        per_device,
        mesh=mesh,
        in_specs=(
            P("mp", None, None),
            P("dp", "mp"),
            P("dp", "mp"),
            P(None, ("dp", "mp")),
            P(None, "mp", "dp"),
            P("mp", None),
        ),
        out_specs=(P("dp", "mp"), P("mp", "dp", None, None)),
        check_vma=False,
    )
```

time: 687 us -> 1900 us (2.77)
  waiting for transfers between devices: 468 us -> 1800 us
  Pallas kernels: 0 us -> 65.8 us
  local copies, waits for them, and re-layouts: 80.1 us -> 14.7 us
  other arithmetic: 59.1 us -> 0 us
  matrix products: 55.9 us -> 0 us
    reduce_scatter x1 -> x2, waiting for transfers between devices: 165 us -> 1430 us  [the longest x1 1270 us: per_device(): lax.psum_scatter(comp, ('dp', 'mp'), scatter_dimension=0, tiled=True)]
    all_gather x2 -> x4, waiting for transfers between devices: 50.9 us -> 361 us  [the longest x1 119 us: per_device(): sketch_t = lax.all_gather(sketch.T, ('dp', 'mp'), tiled=True)]
    psum x1 -> x0, waiting for transfers between devices: 252 us -> none  [per_device(): compressed = lax.psum(compress_part, ('dp', 'mp'))]
    pallas_call x0 -> x2, Pallas kernels: none -> 65.8 us  [the longest x1 42.4 us: local_step(): pl.pallas_call(functools.partial(local_kernel, 1.0 / all_tokens), grid_sp...]
    another operation x9 -> x0, other arithmetic: 53.9 us -> none  [the longest x6 34 us: root_factor(): factor = jnp.linalg.cholesky(shifted_root)]
    dot_general x24 -> x0, matrix products: 53.8 us -> none  [the longest x17 26.2 us: matmul(): jnp.dot(operand_a, operand_b, precision=lax.Precision.HIGHEST, preferred_...]
    div x1 -> x0, local copies, waits for them, and re-layouts: 23.7 us -> none  [per_device(): jnp.einsum('tri,trkn->rikn', hidden_blocks, chosen, preferred_element_typ...]
    gather x4 -> x0, local copies, waits for them, and re-layouts: 19.5 us -> none  [the longest x1 11.4 us: per_device(): jnp.take(cot_blocks, pattern.reshape(-1), axis=1)]
  transfers between devices with their start and end apart: 4 -> 6, of which waited for: 3 -> 6; matrix products, arithmetic and copies ran while one was open for 5% -> 0% of each run, Pallas kernels for 0% -> 0%
where the time goes in v1:
time: 1900 us; the launch traced here: 1890 us
  waiting for transfers between devices  1800 us (95%)
  Pallas kernels  65.8 us (3%)
    reduce_scatter x1, waiting for transfers between devices, per_device(): lax.psum_scatter(comp, ('dp', 'mp'), scatter_dimension=0, tiled=True)  1270 us
    reduce_scatter x1, waiting for transfers between devices, per_device(): grad = lax.psum_scatter(grad, 'dp', scatter_dimension=1, tiled=True)  163 us
    all_gather x1, waiting for transfers between devices, per_device(): sketch_t = lax.all_gather(sketch.T, ('dp', 'mp'), tiled=True)  119 us
    all_gather x1, waiting for transfers between devices, per_device(): comp_t = lax.all_gather(comp_piece, ('dp', 'mp'), tiled=True)  117 us
    all_gather x1, waiting for transfers between devices, per_device(): lax.all_gather(projection.reshape(rank, dev_rows).T, 'dp', tiled=True)  75.4 us
    all_gather x1, waiting for transfers between devices, per_device(): cot = lax.all_gather(cotangent, 'mp')  49.9 us
    pallas_call x1, Pallas kernels, local_step(): pl.pallas_call(functools.partial(local_kernel, 1.0 / all_tokens), grid_sp...  42.4 us
  transfers between devices with their start and end apart: 6, of which 6 were waited for; matrix products, arithmetic and copies ran while one was open for 0% of the time, Pallas kernels for 0%

profile of v1, /device:TPU:1, one launch (start us, length us, event | category | flops | bytes accessed | tf_op | source)
XLA Modules:
  0.0 1891.6 jit_solution(4310459505431018746)
XLA Ops:
  7.2 0.0 all-gather.6.cloned.1.call-start
  7.2 0.7 all-gather.6.cloned.1.call-update
  7.9 0.0 all-gather.12.cloned.1.call-start
  7.9 0.7 all-gather.12.cloned.1.call-update
  8.6 0.0 reduce-scatter.5.cloned.1.call-start
  8.7 0.8 copy.9.pat_ref
  9.5 7.1 copy.12
  16.6 75.4 %all-gather.6.cloned.1.call-done.proj_ref = f32[3584,128]{1,0:T(8,128)} async-done(((f32[56,128]{1,0:T(8,128)}), f32[3584,128]{1,0:T(8,128)}) %all-gather.6.cloned.1.call-update) | async-done | bytes 1835024 | tf_op jit(solution)/shard_map/all_gather | solution.py:232
  92.0 49.9 %all-gather.12.cloned.1.call-done = bf16[1024,2048]{1,0:T(8,128)(2,1)} async-done(((bf16[256,2048]{1,0:T(8,128)(2,1)}), bf16[1024,2048]{1,0:T(8,128)(2,1)}) %all-gather.12.cloned.1.call-update) | async-done | bytes 4194320 | tf_op jit(solution)/shard_map/all_gather | solution.py:231
  141.9 1.5 copy-done.3
  143.4 42.4 %local_step.1 = (bf16[256,3584]{1,0:T(8,128)(2,1)}, f32[8,3584,128]{2,1,0:T(8,128)}, f32[64,128,128]{2,1,0:T(8,128)}) custom-call(s32[28,8]{1,0:T(8,128)S(1)} %copy.9.pat_ref, bf16[4,256,2048]{2,1,0:T(8,128)(2,1)} %bitcast.15, bf16[256,3584]{1,0:T(8,128)(2,1)S(1)} %copy-done.2, bf16[8,3584,128]{2,1,0:T(8,128)(2,1)} %bitcast.11, f32[3584,128]{1,0:T(8,128)S(1)} %copy-done.3), custom_call_target="tpu_custom_call" | custom-call | flops 6000000000 | bytes 36000000 | tf_op jit(solution)/shard_map/local_step/pallas_call | solution.py:101
  185.9 0.0 all-gather.8.cloned.1.call-start
  185.9 0.5 all-gather.8.cloned.1.call-update
  186.4 0.0 all-gather.10.cloned.1.call-start
  186.5 1269.7 %reduce-scatter.5.cloned.1.call-done = f32[32,128]{1,0:T(8,128)} async-done(((f32[8192,128]{1,0:T(8,128)}), f32[32,128]{1,0:T(8,128)}) %reduce-scatter.5.cloned.1.call-update) | async-done | bytes 16400 | tf_op jit(solution)/shard_map/reduce_scatter | solution.py:237
  1456.2 0.0 reduce-scatter.3.cloned.1.call-start
  1456.2 0.5 reduce-scatter.3.cloned.1.call-update
  1456.8 119.3 %all-gather.8.cloned.1.call-done.sketch_ref = f32[8192,128]{1,0:T(8,128)} async-done(((f32[32,128]{1,0:T(8,128)}), f32[8192,128]{1,0:T(8,128)}) %all-gather.8.cloned.1.call-update) | async-done | bytes 4194320 | tf_op jit(solution)/shard_map/all_gather | solution.py:233
  1576.1 116.6 %all-gather.10.cloned.1.call-done.comp_ref = f32[8192,128]{1,0:T(8,128)} async-done(((f32[32,128]{1,0:T(8,128)}), f32[8192,128]{1,0:T(8,128)}) %all-gather.10.cloned.1.call-update) | async-done | bytes 4194320 | tf_op jit(solution)/shard_map/all_gather | solution.py:238
  1692.7 163.3 %reduce-scatter.3.cloned.1.call-done.grad_ref = f32[8,56,128]{2,1,0:T(8,128)} async-done(((f32[8,3584,128]{2,1,0:T(8,128)}), f32[8,56,128]{2,1,0:T(8,128)}) %reduce-scatter.3.cloned.1.call-update) | async-done | bytes 229392 | tf_op jit(solution)/shard_map/reduce_scatter | solution.py:239
  1856.0 2.2 copy-done
  1858.2 2.2 copy-done.1
  1860.4 0.9 copy-done.4
  1861.4 23.4 %finish.1 = f32[56,8,128]{2,1,0:T(8,128)} custom-call(s32[1]{0:T(128)} %bitcast.4.row_ref, s32[28,8]{1,0:T(8,128)S(1)} %copy.9.pat_ref, f32[8,56,128]{2,1,0:T(8,128)S(1)} %copy-done.4, f32[8192,128]{1,0:T(8,128)S(1)} %copy-done, f32[8192,128]{1,0:T(8,128)S(1)} %copy-done.1), custom_call_target="tpu_custom_call" | custom-call | flops 5000000000 | bytes 9000000 | tf_op jit(solution)/shard_map/finish/pallas_call | solution.py:210
  (8 shorter events, 0.0 us)
Async XLA Ops:
  7.2 84.8 %all-gather.6.cloned.1.call-start = ((), (), s32[]{:S(2)}) async-start(), calls=%async_computation.2 | async-start | bytes 1863680 | tf_op jit(solution)/shard_map/all_gather | solution.py:232
  7.9 134.0 %all-gather.12.cloned.1.call-start = ((), (), s32[]{:S(2)}) async-start(), calls=%async_computation.7 | async-start | bytes 5242880 | tf_op jit(solution)/shard_map/all_gather | solution.py:231
  8.6 1447.5 %reduce-scatter.5.cloned.1.call-start = ((), (), s32[]{:S(2)}) async-start(), calls=%async_computation.5 | async-start | bytes 4210688 | tf_op jit(solution)/shard_map/reduce_scatter | solution.py:237
  9.5 132.4 %copy-start.2 = (bf16[256,3584]{1,0:T(8,128)(2,1)S(1)}, bf16[256,3584]{1,0:T(8,128)(2,1)}, u32[]{:S(2)}) copy-start(bf16[256,3584]{1,0:T(8,128)(2,1)} %hid_ref.1) | copy-start | bytes 5505028
  141.9 1.5 copy-start.3
  185.9 1390.2 %all-gather.8.cloned.1.call-start = ((), (), s32[]{:S(2)}) async-start(), calls=%async_computation.4 | async-start | bytes 4210688 | tf_op jit(solution)/shard_map/all_gather | solution.py:233
  186.4 1506.3 %all-gather.10.cloned.1.call-start = ((), (), s32[]{:S(2)}) async-start(), calls=%async_computation.6 | async-start | bytes 4210688 | tf_op jit(solution)/shard_map/all_gather | solution.py:238
  1456.2 399.9 %reduce-scatter.3.cloned.1.call-start = ((), (), s32[]{:S(2)}) async-start(), calls=%async_computation.3 | async-start | bytes 14909440 | tf_op jit(solution)/shard_map/reduce_scatter | solution.py:239
  1856.0 2.2 copy-start
  1858.2 2.2 copy-start.1
  1860.4 0.9 copy-start.4
Sparse Core Ops, SparseCore 0:
  10.7 81.2 all-gather.5
  93.8 48.0 all-gather.11
  186.0 1270.1 reduce-scatter.4
  1460.3 115.7 all-gather.7
  1580.3 112.3 all-gather.9
  1697.5 158.4 reduce-scatter.2

commit v2 on v1

--- a/solution.py
+++ b/solution.py
@@ -27,89 +27,503 @@
     )
 
 
-def local_kernel(inv_tokens, pat_ref, cot_ref, hid_ref, wgt_ref, proj_ref, back_ref, grad_ref, comp_ref, z_ref):
+def local_kernel(inv_tokens, core_ref, pat_ref, cot_ref, hid_ref, wgt_ref, proj_ref, back_ref, grad_ref, comp_ref, z_ref):
     step = pl.program_id(0)
+    core = core_ref[0]
     slots = wgt_ref.shape[0]
+    mine = slots // 2
     blk = hid_ref.shape[1]
+    rank = proj_ref.shape[1]
+    tokens = back_ref.shape[0]
     per_part = cot_ref.shape[2] // blk
-    col_blocks = cot_ref.shape[0] * per_part
-
-    def cot_block(col):
+    half_blocks = z_ref.shape[0]
+    own = pl.ds(pl.multiple_of(core * tokens, tokens), tokens)
+
+    def cot_block(col, rows=slice(None)):
         lane = pl.multiple_of(lax.rem(col, per_part) * blk, blk)
-        return cot_ref[lax.div(col, per_part), :, pl.ds(lane, blk)]
+        return cot_ref[lax.div(col, per_part), rows, pl.ds(lane, blk)]
 
     @pl.when(step == 0)
     def _():
-        @pl.loop(0, col_blocks)
-        def _(col):
-            z_ref[col] = jnp.zeros(z_ref.shape[1:], F32)
+        @pl.loop(0, half_blocks)
+        def _(i):
+            z_ref[i] = jnp.zeros(z_ref.shape[1:], F32)
 
     cols = [pat_ref[step, k] for k in range(slots)]
-    chosen = jnp.concatenate([cot_block(col) for col in cols], axis=1)
+    chosen = jnp.concatenate([cot_block(col, own) for col in cols], axis=1)
     weight = jnp.concatenate([wgt_ref[k] for k in range(slots)], axis=1)
     back = lax.dot_general(chosen, weight, (((1,), (1,)), ((), ())), preferred_element_type=F32)
     back_ref[...] = back.astype(BF16)
     hid = hid_ref[...]
-    grad = lax.dot_general(hid, chosen, (((0,), (0,)), ((), ())), preferred_element_type=F32)
+    wide = jnp.concatenate([cot_block(pat_ref[step, mine * core + j]) for j in range(mine)], axis=1)
+    grad = lax.dot_general(hid, wide, (((0,), (0,)), ((), ())), preferred_element_type=F32)
     grad = grad * inv_tokens
-    for k in range(slots):
-        grad_ref[k] = grad[:, k * blk : (k + 1) * blk]
+    for j in range(mine):
+        grad_ref[j] = grad[:, j * blk : (j + 1) * blk]
     high, low = split_bf16(proj_ref[...])
     both = jnp.dot(hid, jnp.concatenate([high, low], axis=1), preferred_element_type=F32)
-    rank = proj_ref.shape[1]
     y = both[:, :rank] + both[:, rank:]
     for col in cols:
-        z_ref[col] += y
+
+        @pl.when(lax.rem(col, 2) == core)
+        def _(col=col):
+            z_ref[lax.div(col, 2)] += y
 
     @pl.when(step == pl.num_programs(0) - 1)
     def _():
-        @pl.loop(0, col_blocks)
-        def _(col):
-            zh, zl = split_bf16(z_ref[col])
+        @pl.loop(0, half_blocks)
+        def _(i):
+            zh, zl = split_bf16(z_ref[i])
             out = lax.dot_general(
-                cot_block(col),
+                cot_block(2 * i + core),
                 jnp.concatenate([zh, zl], axis=1),
                 (((0,), (0,)), ((), ())),
                 preferred_element_type=F32,
             )
-            comp_ref[col] = (out[:, :rank] + out[:, rank:]) * inv_tokens
-
-
-def local_step(pattern, cot, hidden, weights, proj, all_tokens):
-    parts, tokens, part_cols = cot.shape
+            comp_ref[i] = (out[:, :rank] + out[:, rank:]) * inv_tokens
+
+
+def local_step(core, pattern, cot, hidden, weights, proj, all_tokens):
+    parts, wide_tokens, part_cols = cot.shape
+    tokens = wide_tokens // 2
     block_rows, slots = pattern.shape
     blk = weights.shape[2]
     rows = hidden.shape[1]
     rank = proj.shape[1]
-    col_blocks = parts * part_cols // blk
+    half_blocks = parts * part_cols // blk // 2
     grid_spec = pltpu.PrefetchScalarGridSpec(
-        num_scalar_prefetch=1,
+        num_scalar_prefetch=2,
         grid=(block_rows,),
         in_specs=[
-            pl.BlockSpec((parts, tokens, part_cols), lambda r, pat: (0, 0, 0), pipeline_mode=pl.Buffered(1)),
-            pl.BlockSpec((tokens, blk), lambda r, pat: (0, r)),
-            pl.BlockSpec((slots, blk, blk), lambda r, pat: (0, r, 0)),
-            pl.BlockSpec((blk, rank), lambda r, pat: (r, 0)),
+            pl.BlockSpec((parts, wide_tokens, part_cols), lambda r, *_: (0, 0, 0), pipeline_mode=pl.Buffered(1)),
+            pl.BlockSpec((wide_tokens, blk), lambda r, *_: (0, r)),
+            pl.BlockSpec((slots, blk, blk), lambda r, *_: (0, r, 0)),
+            pl.BlockSpec((blk, rank), lambda r, *_: (r, 0)),
         ],
         out_specs=[
-            pl.BlockSpec((tokens, blk), lambda r, pat: (0, r)),
-            pl.BlockSpec((slots, blk, blk), lambda r, pat: (0, r, 0)),
-            pl.BlockSpec((col_blocks, blk, rank), lambda r, pat: (0, 0, 0), pipeline_mode=pl.Buffered(1)),
+            pl.BlockSpec((tokens, blk), lambda r, *_: (0, r)),
+            pl.BlockSpec((slots // 2, blk, blk), lambda r, *_: (0, r, 0)),
+            pl.BlockSpec((half_blocks, blk, rank), lambda r, *_: (0, 0, 0), pipeline_mode=pl.Buffered(1)),
         ],
-        scratch_shapes=[pltpu.VMEM((col_blocks, tokens, rank), F32)],
+        scratch_shapes=[pltpu.VMEM((half_blocks, wide_tokens, rank), F32)],
     )
     return pl.pallas_call(
         functools.partial(local_kernel, 1.0 / all_tokens),
         grid_spec=grid_spec,
         out_shape=(
             jax.ShapeDtypeStruct((tokens, rows), BF16),
-            jax.ShapeDtypeStruct((slots, rows, blk), F32),
-            jax.ShapeDtypeStruct((col_blocks, blk, rank), F32),
+            jax.ShapeDtypeStruct((slots // 2, rows, blk), F32),
+            jax.ShapeDtypeStruct((half_blocks, blk, rank), F32),
         ),
         compiler_params=pltpu.CompilerParams(vmem_limit_bytes=48 * MIB),
         cost_estimate=pl.CostEstimate(flops=6_000_000_000, bytes_accessed=36_000_000, transcendentals=0),
         name="local_step",
-    )(pattern, cot, hidden, weights, proj)
+    )(core, pattern, cot, hidden, weights, proj)
+
+
+class Wires:
+    def __init__(self, send_sems, recv_sems, local_sems):
+        self.send_sems, self.recv_sems, self.local_sems = send_sems, recv_sems, local_sems
+        self.used = 0
+        self.locals = 0
+        self.sent = []
+
+    def send(self, source, target, device):
+        copy = pltpu.make_async_remote_copy(
+            src_ref=source,
+            dst_ref=target,
+            send_sem=self.send_sems.at[self.used],
+            recv_sem=self.recv_sems.at[self.used],
+            device_id=device,
+            device_id_type=pl.DeviceIdType.MESH,
+        )
+        self.used += 1
+        copy.start()
+        self.sent.append(copy)
+        return copy
+
+    def keep(self, source, target):
+        copy = pltpu.make_async_copy(source, target, self.local_sems.at[self.locals])
+        self.locals += 1
+        copy.start()
+        return copy
+
+    def drain(self):
+        for copy in self.sent:
+            copy.wait_send()
+
+
+def received(*copies):
+    for copy in copies:
+        copy.wait_recv()
+
+
+class Place:
+    def __init__(self, ny, nz, nx):
+        self.n = {"x": nx, "y": ny, "z": nz, "c": 2}
+        d = lax.axis_index("dp")
+        self.at = {
+            "x": lax.axis_index("mp"),
+            "c": lax.rem(d, 2),
+            "y": lax.rem(lax.div(d, 2), ny),
+            "z": lax.div(d, 2 * ny),
+        }
+
+    def shift(self, axis, by):
+        n = self.n[axis]
+        return lax.rem(self.at[axis] + (by % n), n)
+
+    def device(self, axis, by):
+        at = dict(self.at)
+        at[axis] = self.shift(axis, by)
+        return ((at["z"] * self.n["y"] + at["y"]) * 2 + at["c"], at["x"])
+
+
+def meet(devices):
+    barrier = pltpu.get_barrier_semaphore()
+    for device in devices:
+        pl.semaphore_signal(barrier, inc=1, device_id=device, device_id_type=pl.DeviceIdType.MESH)
+    pl.semaphore_wait(barrier, len(devices))
+
+
+def gather_kernel(ny, nz, nx, cot, hid, proj, sk, cot_o, hid_o, proj_o, sk_o, send_sems, recv_sems, local_sems):
+    here = Place(ny, nz, nx)
+    x, y, z, c = (here.at[name] for name in "xyzc")
+    wires = Wires(send_sems, recv_sems, local_sems)
+    partners = [here.device("x", j) for j in range(1, nx)] + [here.device("y", j) for j in range(1, ny)]
+    partners += [here.device("z", 1), here.device("z", -1), here.device("c", 1)]
+    sib = here.device("c", 1)
+    keep_sk = wires.keep(sk, sk_o.at[z, y, c, x])
+    keep_proj = wires.keep(proj, proj_o.at[z, y, c])
+    keep_cot = wires.keep(cot, cot_o.at[x, c])
+    keep_hid = wires.keep(hid, hid_o.at[c])
+    meet(partners)
+    rows = cot.shape[0] // 2
+    top, bottom = pl.ds(0, rows), pl.ds(rows, rows)
+    sk_x = [wires.send(sk, sk_o.at[z, y, c, x], here.device("x", j)) for j in range(1, nx)]
+    proj_y = [wires.send(proj, proj_o.at[z, y, c], here.device("y", j)) for j in range(1, ny)]
+    right, left = here.device("x", 1), here.device("x", -1)
+
+    def cot_send(rows_at, device):
+        return wires.send(cot.at[rows_at], cot_o.at[x, c, rows_at], device)
+
+    def cot_pass(part, rows_at, device):
+        return wires.send(cot_o.at[part, c, rows_at], cot_o.at[part, c, rows_at], device)
+
+    r_top, l_bottom = cot_send(top, right), cot_send(bottom, left)
+    r_bottom, l_top = cot_send(bottom, right), cot_send(top, left)
+    from_sib = [wires.send(hid, hid_o.at[c], sib), wires.send(cot, cot_o.at[x, c], sib)]
+
+    keep_sk.wait()
+    received(*sk_x)
+    sk_y = [
+        wires.send(sk_o.at[z, y, c], sk_o.at[z, y, c], here.device("y", j)) for j in range(1, ny)
+    ]
+    keep_proj.wait()
+    received(*proj_y)
+
+    up, down = here.device("z", 1), here.device("z", -1)
+
+    def z_pass(ref, layer, device, ys=slice(None)):
+        view = ref.at[layer, ys, c]
+        return wires.send(view, view, device)
+
+    arrays = (proj_o, sk_o)
+    low, high = pl.ds(0, ny // 2), pl.ds(ny // 2, ny // 2)
+    going_up, going_down = [z_pass(proj_o, z, up)], [z_pass(proj_o, z, down)]
+    from_sib.append(z_pass(proj_o, z, sib))
+    received(*sk_y)
+    going_up.append(z_pass(sk_o, z, up))
+    going_down.append(z_pass(sk_o, z, down))
+    from_sib.append(z_pass(sk_o, z, sib))
+
+    def z_step(distance, going_up, going_down):
+        below, above = here.shift("z", -distance), here.shift("z", distance)
+        next_up, next_down = [], []
+        last = distance == nz // 2
+        for moved, layer, device, part, nexts in (
+            (going_up, below, up, low, next_up),
+            (going_down, above, down, high, next_down),
+        ):
+            for copy, ref in zip(moved, arrays):
+                received(copy)
+                if not last:
+                    ys = part if distance + 1 == nz // 2 else slice(None)
+                    nexts.append(z_pass(ref, layer, device, ys))
+                from_sib.append(z_pass(ref, layer, sib, part if last else slice(None)))
+        return next_up, next_down
+
+    left_part, right_part, far_part = here.shift("x", -1), here.shift("x", 1), here.shift("x", 2)
+
+    def cot_first():
+        received(r_top)
+        far_top = cot_pass(left_part, top, right)
+        from_sib.append(cot_pass(left_part, top, sib))
+        received(l_bottom)
+        far_bottom = cot_pass(right_part, bottom, left)
+        from_sib.append(cot_pass(right_part, bottom, sib))
+        return far_top, far_bottom
+
+    for distance in range(1, nz // 2 + 1):
+        if distance == 2:
+            far_top, far_bottom = cot_first()
+        if distance == 3:
+            received(r_bottom)
+            from_sib.append(cot_pass(left_part, bottom, sib))
+            received(l_top)
+            from_sib.append(cot_pass(right_part, top, sib))
+        going_up, going_down = z_step(distance, going_up, going_down)
+    received(far_top)
+    from_sib.append(cot_pass(far_part, top, sib))
+    received(far_bottom)
+    from_sib.append(cot_pass(far_part, bottom, sib))
+    keep_cot.wait()
+    keep_hid.wait()
+    received(*from_sib)
+    wires.drain()
+
+
+def gather(ny, nz, nx, cot, hid, proj, sk):
+    any_spec = pl.BlockSpec(memory_space=pl.ANY)
+    copies = 80
+    return pl.pallas_call(
+        functools.partial(gather_kernel, ny, nz, nx),
+        in_specs=[any_spec] * 4,
+        out_specs=[any_spec] * 4,
+        out_shape=(
+            jax.ShapeDtypeStruct((nx, 2) + cot.shape, cot.dtype),
+            jax.ShapeDtypeStruct((2,) + hid.shape, hid.dtype),
+            jax.ShapeDtypeStruct((nz, ny, 2) + proj.shape, proj.dtype),
+            jax.ShapeDtypeStruct((nz, ny, 2, nx) + sk.shape, sk.dtype),
+        ),
+        scratch_shapes=[
+            pltpu.SemaphoreType.DMA((copies,)),
+            pltpu.SemaphoreType.DMA((copies,)),
+            pltpu.SemaphoreType.DMA((4,)),
+        ],
+        compiler_params=pltpu.CompilerParams(collective_id=1, has_side_effects=True),
+        cost_estimate=pl.CostEstimate(flops=0, bytes_accessed=60_000_000, transcendentals=0),
+        name="gather",
+    )(cot, hid, proj, sk)
+
+
+def add_into(target, index, source, loop):
+    at = index.index(None)
+
+    @pl.loop(0, loop)
+    def _(i):
+        place = tuple(index[:at]) + (i,) + tuple(index[at + 1 :])
+        target[place] = target[place] + source[i]
+
+
+def reduce_kernel(
+    ny, nz, nx, grad, comp, grad_o, comp_o, xg, xc, ya, za, zb, yb, cx, cy, cz, send_sems, recv_sems, local_sems
+):
+    here = Place(ny, nz, nx)
+    x, y, z, c = (here.at[name] for name in "xyzc")
+    wires = Wires(send_sems, recv_sems, local_sems)
+    keep_comp = wires.keep(comp, xc)
+    keep_grad = wires.keep(grad, xg)
+    sib = here.device("c", 1)
+    partners = [here.device("x", j) for j in range(1, nx)] + [here.device("y", j) for j in range(1, ny)]
+    partners += [here.device("z", j) for j in range(1, nz)] + [sib]
+    meet(partners)
+    xp, xm = here.device("x", 1), here.device("x", -1)
+    yp, ym = here.device("y", 1), here.device("y", -1)
+    zp, zm = here.device("z", 1), here.device("z", -1)
+    x1, x2, x3 = (here.shift("x", j) for j in (1, 2, 3))
+    y1, y2, y3 = (here.shift("y", j) for j in (1, 2, 3))
+    send = wires.send
+    zlow, zhigh = pl.ds(0, nz // 2), pl.ds(nz // 2, nz // 2)
+
+    keep_comp.wait()
+    c_far = (
+        send(xc.at[zlow, :, x2], cx.at[0, zlow], xp),
+        send(xc.at[zhigh, :, x2], cx.at[1, zhigh], xm),
+    )
+    c_near = [
+        send(xc.at[zhigh, :, x1], cx.at[2, zhigh], xp),
+        send(xc.at[zlow, :, x3], cx.at[3, zlow], xm),
+    ]
+    keep_grad.wait()
+    a_far = (send(xg.at[0, :, y2], ya.at[0], yp), send(xg.at[1, :, y2], ya.at[1], ym))
+    b_dist = nz // 2
+
+    def b_send(slot_at, dist):
+        first = slot_at == "far"
+        plus = here.shift("z", dist)
+        minus = here.shift("z", -dist)
+        if first:
+            return (
+                [send(xg.at[2, plus], zb.at[0, dist - 1, 0], zp)],
+                [send(xg.at[3, minus], zb.at[1, dist - 1, 1], zm)],
+            )
+        return (
+            [send(xg.at[pl.ds(2, 2), plus], zb.at[0, dist - 1], zp)],
+            [send(xg.at[pl.ds(2, 2), minus], zb.at[1, dist - 1], zm)],
+        )
+
+    b_moving = b_send("far", b_dist)
+    a_near = [send(xg.at[1, :, y1], ya.at[2], yp), send(xg.at[0, :, y3], ya.at[3], ym)]
+
+    def b_step(dist, moving):
+        for side, slots in ((0, (0,) if dist == b_dist else (0, 1)), (1, (1,) if dist == b_dist else (0, 1))):
+            received(*moving[side])
+            layer = here.shift("z", (dist - 1) * (1 - 2 * side))
+            for s in slots:
+                add_into(xg, [2 + s, layer, None], zb.at[side, dist - 1, s], ny)
+        return b_send("near", dist - 1) if dist > 1 else None
+
+    b_moving = b_step(b_dist, b_moving)
+    received(c_far[0])
+    add_into(xc, [None, slice(None), x1], cx.at[0], nz // 2)
+    c_near.append(send(xc.at[zlow, :, x1], cx.at[2, zlow], xp))
+    received(c_far[1])
+
+    @pl.loop(nz // 2, nz)
+    def _(i):
+        xc[i, :, x3] = xc[i, :, x3] + cx[1, i]
+
+    c_near.append(send(xc.at[zhigh, :, x3], cx.at[3, zhigh], xm))
+    received(a_far[0])
+    add_into(xg, [0, None, y1], ya.at[0], nz)
+    a_near.append(send(xg.at[0, :, y1], ya.at[4], yp))
+    received(a_far[1])
+    add_into(xg, [1, None, y3], ya.at[1], nz)
+    a_near.append(send(xg.at[1, :, y3], ya.at[5], ym))
+    b_moving = b_step(3, b_moving)
+
+    received(*c_near)
+
+    @pl.loop(0, nz)
+    def _(i):
+        xc[i, :, x] = xc[i, :, x] + cx[2, i] + cx[3, i]
+
+    c_y = [send(xc.at[:, here.shift("y", j), x], cy.at[j - 1], here.device("y", j)) for j in range(1, ny)]
+    received(*c_y)
+
+    @pl.loop(0, nz)
+    def _(i):
+        xc[i, y, x] = xc[i, y, x] + (cy[0, i] + cy[1, i] + cy[2, i])
+
+    c_z = [send(xc.at[here.shift("z", j), y, x], cz.at[j - 1], here.device("z", j)) for j in range(1, nz)]
+    b_moving = b_step(2, b_moving)
+    received(*c_z)
+    total = xc[z, y, x]
+    for j in range(nz - 1):
+        total = total + cz[j]
+    comp_o[z, y, c, x] = total
+    mine = comp_o.at[z, y, c, x]
+    g_z = [send(mine, mine, here.device("z", j)) for j in range(1, nz)]
+    received(*a_near)
+
+    @pl.loop(0, nz)
+    def _(i):
+        xg[0, i, y] = xg[0, i, y] + ya[2 + 2, i] + ya[3, i]
+        xg[1, i, y] = xg[1, i, y] + ya[2, i] + ya[5, i]
+
+    def a_send(dist):
+        plus, minus = here.shift("z", dist), here.shift("z", -dist)
+        if dist == b_dist:
+            return (
+                [send(xg.at[0, plus, y], za.at[0, dist - 1, 0], zp)],
+                [send(xg.at[1, minus, y], za.at[1, dist - 1, 1], zm)],
+            )
+        return (
+            [send(xg.at[pl.ds(0, 2), plus, y], za.at[0, dist - 1], zp)],
+            [send(xg.at[pl.ds(0, 2), minus, y], za.at[1, dist - 1], zm)],
+        )
+
+    def a_step(dist, moving):
+        for side, slots in ((0, (0,) if dist == b_dist else (0, 1)), (1, (1,) if dist == b_dist else (0, 1))):
+            received(*moving[side])
+            layer = here.shift("z", (dist - 1) * (1 - 2 * side))
+            for s in slots:
+                xg[s, layer, y] = xg[s, layer, y] + za[side, dist - 1, s]
+        return a_send(dist - 1) if dist > 1 else None
+
+    a_moving = a_send(b_dist)
+    received(*g_z)
+    column = comp_o.at[:, y, c, x]
+    g_y = [send(column, column, here.device("y", j)) for j in range(1, ny)]
+    b_step(1, b_moving)
+    b2_far = (send(xg.at[2, z, y2], yb.at[0], yp), send(xg.at[3, z, y2], yb.at[1], ym))
+    b2_near = [send(xg.at[3, z, y1], yb.at[2], yp), send(xg.at[2, z, y3], yb.at[3], ym)]
+    received(*g_y)
+    plane = comp_o.at[:, :, c, x]
+    g_x = (send(plane, plane, xp), send(plane, plane, xm))
+    from_sib = [send(plane, plane, sib)]
+    a_moving = a_step(b_dist, a_moving)
+    received(b2_far[0])
+    xg[2, z, y1] = xg[2, z, y1] + yb[0]
+    b2_near.append(send(xg.at[2, z, y1], yb.at[4], yp))
+    received(b2_far[1])
+    xg[3, z, y3] = xg[3, z, y3] + yb[1]
+    b2_near.append(send(xg.at[3, z, y3], yb.at[5], ym))
+    a_moving = a_step(3, a_moving)
+    a_moving = a_step(2, a_moving)
+    received(*b2_near)
+    xg[2, z, y] = xg[2, z, y] + yb[4] + yb[3]
+    xg[3, z, y] = xg[3, z, y] + yb[2] + yb[5]
+    a_step(1, a_moving)
+    units = grad_o.shape[1]
+    theirs = pl.ds(pl.multiple_of((1 - c) * units, 8), units)
+    swap = send(xg.at[:, z, y, theirs], grad_o.at[pl.ds(c * 4, 4)], sib)
+    for s in range(4):
+        grad_o[c * 4 + s] = xg[s, z, y, pl.ds(pl.multiple_of(c * units, 8), units)]
+    received(g_x[0])
+    part = comp_o.at[zlow, :, c, x3]
+    far = [send(part, part, xp)]
+    received(g_x[1])
+    part = comp_o.at[zhigh, :, c, x1]
+    far.append(send(part, part, xm))
+    for at in (x3, x1):
+        part = comp_o.at[:, :, c, at]
+        from_sib.append(send(part, part, sib))
+    received(far[0])
+    part = comp_o.at[zlow, :, c, x2]
+    from_sib.append(send(part, part, sib))
+    received(far[1])
+    part = comp_o.at[zhigh, :, c, x2]
+    from_sib.append(send(part, part, sib))
+    received(swap, *from_sib)
+    wires.drain()
+
+
+def reduce_all(ny, nz, nx, grad, comp):
+    slots, _, _, units, blk = grad.shape
+    piece = comp.shape[3:]
+    any_spec = pl.BlockSpec(memory_space=pl.ANY)
+    vmem = pl.BlockSpec(memory_space=pltpu.VMEM)
+    copies = 96
+    return pl.pallas_call(
+        functools.partial(reduce_kernel, ny, nz, nx),
+        in_specs=[any_spec] * 2,
+        out_specs=[vmem, vmem],
+        out_shape=(
+            jax.ShapeDtypeStruct((2 * slots, units // 2, blk), F32),
+            jax.ShapeDtypeStruct((nz, ny, 2, nx) + piece, F32),
+        ),
+        scratch_shapes=[
+            pltpu.VMEM(grad.shape, F32),
+            pltpu.VMEM(comp.shape, F32),
+            pltpu.VMEM((6, nz, units, blk), F32),
+            pltpu.VMEM((2, nz // 2, 2, units, blk), F32),
+            pltpu.VMEM((2, nz // 2, 2, ny, units, blk), F32),
+            pltpu.VMEM((6, units, blk), F32),
+            pltpu.VMEM((4, nz, ny) + piece, F32),
+            pltpu.VMEM((ny - 1, nz) + piece, F32),
+            pltpu.VMEM((nz - 1,) + piece, F32),
+            pltpu.SemaphoreType.DMA((copies,)),
+            pltpu.SemaphoreType.DMA((copies,)),
+            pltpu.SemaphoreType.DMA((2,)),
+        ],
+        compiler_params=pltpu.CompilerParams(
+            collective_id=2, has_side_effects=True, vmem_limit_bytes=48 * MIB
+        ),
+        cost_estimate=pl.CostEstimate(flops=0, bytes_accessed=100_000_000, transcendentals=0),
+        name="reduce",
+    )(grad, comp)
 
 
 def identity(n):
@@ -226,19 +640,26 @@
     rank = sketch.shape[0]
     slots, blk = weights.shape[1:]
     dp_size = lax.axis_size("dp")
+    nx = lax.axis_size("mp")
+    ny = 4
+    nz = dp_size // (2 * ny)
     dev_rows = weights.shape[0] // dp_size
     all_tokens = hidden.shape[0] * dp_size
-    cot = lax.all_gather(cotangent, "mp")
-    proj = lax.all_gather(projection.reshape(rank, dev_rows).T, "dp", tiled=True)
-    sketch_t = lax.all_gather(sketch.T, ("dp", "mp"), tiled=True)
-    weights_t = weights.transpose(1, 0, 2)
-    input_grad, grad, comp = local_step(pattern, cot, hidden, weights_t, proj, all_tokens)
-    comp = comp.reshape(-1, rank)
-    comp_piece = lax.psum_scatter(comp, ("dp", "mp"), scatter_dimension=0, tiled=True)
-    comp_t = lax.all_gather(comp_piece, ("dp", "mp"), tiled=True)
-    grad = lax.psum_scatter(grad, "dp", scatter_dimension=1, tiled=True)
-    start_row = (lax.axis_index("dp") * dev_rows).reshape(1).astype(jnp.int32)
-    direction = finish(start_row, pattern, grad, sketch_t, comp_t)
+    dp = lax.axis_index("dp")
+    core = lax.rem(dp, 2).reshape(1).astype(jnp.int32)
+    cot, hid, proj, sketch_t = gather(
+        ny, nz, nx, cotangent, hidden, projection.reshape(rank, dev_rows).T, sketch.T
+    )
+    cot = cot.reshape(nx, -1, cotangent.shape[1])
+    hid = hid.reshape(-1, hidden.shape[1])
+    input_grad, grad, comp = local_step(
+        core, pattern, cot, hid, weights.transpose(1, 0, 2), proj.reshape(-1, rank), all_tokens
+    )
+    grad, comp = reduce_all(
+        ny, nz, nx, grad.reshape(slots // 2, nz, ny, 2 * dev_rows, blk), comp.reshape(nz, ny, nx, -1, rank)
+    )
+    start_row = (dp * dev_rows).reshape(1).astype(jnp.int32)
+    direction = finish(start_row, pattern, grad, sketch_t.reshape(-1, rank), comp.reshape(-1, rank))
     return input_grad, direction[None]
 
 

time: 1900 us -> 267 us (0.14)
  waiting for transfers between devices: 1800 us -> 0 us
  Pallas kernels: 65.8 us -> 254 us
    reduce_scatter x2 -> x0, waiting for transfers between devices: 1430 us -> none  [the longest x1 1270 us: per_device(): lax.psum_scatter(comp, ('dp', 'mp'), scatter_dimension=0, tiled=True)]
    all_gather x4 -> x0, waiting for transfers between devices: 361 us -> none  [the longest x1 119 us: per_device(): sketch_t = lax.all_gather(sketch.T, ('dp', 'mp'), tiled=True)]
    pallas_call x0 -> x2, Pallas kernels: none -> 191 us  [the longest x1 99.8 us: reduce_all(): pl.pallas_call(functools.partial(reduce_kernel, ny, nz, nx), in_specs=[an...]
  transfers between devices with their start and end apart: 6 -> 0, of which waited for: 6 -> 0; matrix products, arithmetic and copies ran while one was open for 0% -> 0% of each run, Pallas kernels for 0% -> 0%
where the time goes in v2:
time: 267 us; the launch traced here: 266 us
  Pallas kernels  254 us (95%)
  local copies, waits for them, and re-layouts  11.5 us (4%)
    pallas_call x1, Pallas kernels, reduce_all(): pl.pallas_call(functools.partial(reduce_kernel, ny, nz, nx), in_specs=[an...  99.8 us
    pallas_call x1, Pallas kernels, gather(): pl.pallas_call(functools.partial(gather_kernel, ny, nz, nx), in_specs=[an...  91.4 us
    pallas_call x1, Pallas kernels, local_step(): pl.pallas_call(functools.partial(local_kernel, 1.0 / all_tokens), grid_sp...  39.4 us
    pallas_call x1, Pallas kernels, finish(): pl.pallas_call(finish_kernel, in_specs=[smem, smem, vmem, vmem, vmem], ou...  23.4 us
    unnamed x8, local copies, waits for them, and re-layouts  11.5 us

profile of v2, /device:TPU:1, one launch (start us, length us, event | category | flops | bytes accessed | tf_op | source)
XLA Modules:
  0.0 266.2 jit_solution(8741543897779504719)
XLA Ops:
  0.6 0.8 copy.9.pat_ref
  1.4 7.0 %copy.12 = bf16[3584,8,128]{2,0,1:T(8,128)(2,1)} copy(bf16[3584,8,128]{2,1,0:T(8,128)(2,1)} %param.6) | data formatting | bytes 14680064 | tf_op args[0]
  8.4 91.4 %gather.1 = (bf16[4,2,256,2048]{3,2,1,0:T(8,128)(2,1)}, bf16[2,256,3584]{2,1,0:T(8,128)(2,1)}, f32[8,4,2,56,128]{4,3,2,1,0:T(8,128)}, f32[8,4,2,4,32,128]{5,4,3,2,1,0:T(8,128)}) custom-call(bf16[256,2048]{1,0:T(8,128)(2,1)} %cot.1, bf16[256,3584]{1,0:T(8,128)(2,1)} %hid.1, f32[56,128]{1,0:T(8,128)} %bitcast.23, f32[32,128]{1,0:T(8,128)} %bitcast.24), custom_call_target="tpu_custom_call" | custom-call | bytes 60000000 | tf_op jit(solution)/shard_map/gather/pallas_call | solution.py:289
  99.9 0.0 copy-start.2
  99.9 1.5 copy-done.2
  101.4 39.4 %local_step.1 = (bf16[256,3584]{1,0:T(8,128)(2,1)}, f32[4,3584,128]{2,1,0:T(8,128)}, f32[32,128,128]{2,1,0:T(8,128)S(1)}) custom-call(s32[1]{0:T(128)} %bitcast.core_ref, s32[28,8]{1,0:T(8,128)S(1)} %copy.9.pat_ref, bf16[4,512,2048]{2,1,0:T(8,128)(2,1)} %bitcast.25, bf16[512,3584]{1,0:T(8,128)(2,1)} %bitcast.26, bf16[8,3584,128]{2,1,0:T(8,128)(2,1)} %bitcast.21, ...), custom_call_target="tpu_custom_call" | custom-call | flops 6000000000 | bytes 36000000 | tf_op jit(solution)/shard_map/local_step/pallas_call | solution.py:110
  140.8 0.0 copy-start
  140.8 99.8 %reduce.1 = (f32[8,56,128]{2,1,0:T(8,128)S(1)}, f32[8,4,2,4,32,128]{5,4,3,2,1,0:T(8,128)}) custom-call(f32[4,8,4,112,128]{4,3,2,1,0:T(8,128)} %bitcast.22, f32[8,4,4,32,128]{4,3,2,1,0:T(8,128)S(1)} %bitcast.17), custom_call_target="tpu_custom_call" | custom-call | bytes 100000000 | tf_op jit(solution)/shard_map/reduce/pallas_call | solution.py:499
  240.6 0.0 copy-done
  240.6 0.0 copy-start.1
  240.6 2.2 copy-done.1
  242.8 23.4 %finish.1 = f32[56,8,128]{2,1,0:T(8,128)} custom-call(s32[1]{0:T(128)} %bitcast.8.row_ref, s32[28,8]{1,0:T(8,128)S(1)} %copy.9.pat_ref, f32[8,56,128]{2,1,0:T(8,128)S(1)} %get-tuple-element.17.grad_ref, f32[8192,128]{1,0:T(8,128)S(1)} %bitcast.18, f32[8192,128]{1,0:T(8,128)S(1)} %bitcast.19), custom_call_target="tpu_custom_call" | custom-call | flops 5000000000 | bytes 9000000 | tf_op jit(solution)/shard_map/finish/pallas_call | solution.py:624
Async XLA Ops:
  99.9 1.5 copy-start.2
  140.8 99.8 %copy-start = (f32[8,4,2,4,32,128]{5,4,3,2,1,0:T(8,128)S(1)}, f32[8,4,2,4,32,128]{5,4,3,2,1,0:T(8,128)}, u32[]{:S(2)}) copy-start(f32[8,4,2,4,32,128]{5,4,3,2,1,0:T(8,128)} %get-tuple-element.18) | copy-start | bytes 12582916
  240.6 2.2 copy-start.1

commit v3 on v2

--- a/solution.py
+++ b/solution.py
@@ -186,18 +186,16 @@
     pl.semaphore_wait(barrier, len(devices))
 
 
-def gather_kernel(ny, nz, nx, cot, hid, proj, sk, cot_o, hid_o, proj_o, sk_o, send_sems, recv_sems, local_sems):
+def gather_kernel(ny, nz, nx, cot, hid, proj, sk, cot_o, hid_o, proj_o, sk_o, cot_v, hid_v, proj_v, sk_v, send_sems, recv_sems, local_sems):
     here = Place(ny, nz, nx)
     x, y, z, c = (here.at[name] for name in "xyzc")
     wires = Wires(send_sems, recv_sems, local_sems)
     partners = [here.device("x", j) for j in range(1, nx)] + [here.device("y", j) for j in range(1, ny)]
     partners += [here.device("z", 1), here.device("z", -1), here.device("c", 1)]
     sib = here.device("c", 1)
-    keep_sk = wires.keep(sk, sk_o.at[z, y, c, x])
-    keep_proj = wires.keep(proj, proj_o.at[z, y, c])
-    keep_cot = wires.keep(cot, cot_o.at[x, c])
-    keep_hid = wires.keep(hid, hid_o.at[c])
+    loads = [wires.keep(a, b) for a, b in ((sk, sk_v), (proj, proj_v), (cot, cot_v), (hid, hid_v))]
     meet(partners)
+    targets = (sk_o.at[z, y, c, x], proj_o.at[z, y, c], cot_o.at[x, c], hid_o.at[c])
     rows = cot.shape[0] // 2
     top, bottom = pl.ds(0, rows), pl.ds(rows, rows)
     sk_x = [wires.send(sk, sk_o.at[z, y, c, x], here.device("x", j)) for j in range(1, nx)]
@@ -214,6 +212,11 @@
     r_bottom, l_top = cot_send(bottom, right), cot_send(top, left)
     from_sib = [wires.send(hid, hid_o.at[c], sib), wires.send(cot, cot_o.at[x, c], sib)]
 
+    keeps = []
+    for load, value, target in zip(loads, (sk_v, proj_v, cot_v, hid_v), targets):
+        load.wait()
+        keeps.append(wires.keep(value, target))
+    keep_sk, keep_proj, keep_cot, keep_hid = keeps
     keep_sk.wait()
     received(*sk_x)
     sk_y = [
@@ -297,9 +300,13 @@
             jax.ShapeDtypeStruct((nz, ny, 2, nx) + sk.shape, sk.dtype),
         ),
         scratch_shapes=[
+            pltpu.VMEM(cot.shape, cot.dtype),
+            pltpu.VMEM(hid.shape, hid.dtype),
+            pltpu.VMEM(proj.shape, proj.dtype),
+            pltpu.VMEM(sk.shape, sk.dtype),
             pltpu.SemaphoreType.DMA((copies,)),
             pltpu.SemaphoreType.DMA((copies,)),
-            pltpu.SemaphoreType.DMA((4,)),
+            pltpu.SemaphoreType.DMA((8,)),
         ],
         compiler_params=pltpu.CompilerParams(collective_id=1, has_side_effects=True),
         cost_estimate=pl.CostEstimate(flops=0, bytes_accessed=60_000_000, transcendentals=0),

time: 267 us -> 225 us (0.84)
  Pallas kernels: 254 us -> 212 us
    pallas_call x1, Pallas kernels: 91.4 us -> 52.4 us  [gather(): pl.pallas_call(functools.partial(gather_kernel, ny, nz, nx), in_specs=[an...]
    pallas_call x1, Pallas kernels: 99.8 us -> 96.7 us  [reduce_all(): pl.pallas_call(functools.partial(reduce_kernel, ny, nz, nx), in_specs=[an...]
where the time goes in v3:
time: 225 us; the launch traced here: 224 us
  Pallas kernels  212 us (94%)
  local copies, waits for them, and re-layouts  11.5 us (5%)
    pallas_call x1, Pallas kernels, reduce_all(): pl.pallas_call(functools.partial(reduce_kernel, ny, nz, nx), in_specs=[an...  96.7 us
    pallas_call x1, Pallas kernels, gather(): pl.pallas_call(functools.partial(gather_kernel, ny, nz, nx), in_specs=[an...  52.4 us
    pallas_call x1, Pallas kernels, local_step(): pl.pallas_call(functools.partial(local_kernel, 1.0 / all_tokens), grid_sp...  39.4 us
    pallas_call x1, Pallas kernels, finish(): pl.pallas_call(finish_kernel, in_specs=[smem, smem, vmem, vmem, vmem], ou...  23.4 us
    unnamed x8, local copies, waits for them, and re-layouts  11.5 us

profile of v3, /device:TPU:1, one launch (start us, length us, event | category | flops | bytes accessed | tf_op | source)
XLA Modules:
  0.0 224.1 jit_solution(15550962153929680816)
XLA Ops:
  0.6 0.8 copy.9.pat_ref
  1.4 7.0 %copy.12 = bf16[3584,8,128]{2,0,1:T(8,128)(2,1)} copy(bf16[3584,8,128]{2,1,0:T(8,128)(2,1)} %param.6) | data formatting | bytes 14680064 | tf_op args[0]
  8.4 52.4 %gather.1 = (bf16[4,2,256,2048]{3,2,1,0:T(8,128)(2,1)}, bf16[2,256,3584]{2,1,0:T(8,128)(2,1)}, f32[8,4,2,56,128]{4,3,2,1,0:T(8,128)}, f32[8,4,2,4,32,128]{5,4,3,2,1,0:T(8,128)}) custom-call(bf16[256,2048]{1,0:T(8,128)(2,1)} %cot.1, bf16[256,3584]{1,0:T(8,128)(2,1)} %hid.1, f32[56,128]{1,0:T(8,128)} %bitcast.23, f32[32,128]{1,0:T(8,128)} %bitcast.24), custom_call_target="tpu_custom_call" | custom-call | bytes 60000000 | tf_op jit(solution)/shard_map/gather/pallas_call | solution.py:292
  60.9 0.0 copy-start.2
  60.9 1.5 copy-done.2
  62.4 39.4 %local_step.1 = (bf16[256,3584]{1,0:T(8,128)(2,1)}, f32[4,3584,128]{2,1,0:T(8,128)}, f32[32,128,128]{2,1,0:T(8,128)S(1)}) custom-call(s32[1]{0:T(128)} %bitcast.core_ref, s32[28,8]{1,0:T(8,128)S(1)} %copy.9.pat_ref, bf16[4,512,2048]{2,1,0:T(8,128)(2,1)} %bitcast.25, bf16[512,3584]{1,0:T(8,128)(2,1)} %bitcast.26, bf16[8,3584,128]{2,1,0:T(8,128)(2,1)} %bitcast.21, ...), custom_call_target="tpu_custom_call" | custom-call | flops 6000000000 | bytes 36000000 | tf_op jit(solution)/shard_map/local_step/pallas_call | solution.py:110
  101.8 0.0 copy-start
  101.8 96.7 %reduce.1 = (f32[8,56,128]{2,1,0:T(8,128)S(1)}, f32[8,4,2,4,32,128]{5,4,3,2,1,0:T(8,128)}) custom-call(f32[4,8,4,112,128]{4,3,2,1,0:T(8,128)} %bitcast.22, f32[8,4,4,32,128]{4,3,2,1,0:T(8,128)S(1)} %bitcast.17), custom_call_target="tpu_custom_call" | custom-call | bytes 100000000 | tf_op jit(solution)/shard_map/reduce/pallas_call | solution.py:506
  198.5 0.0 copy-done
  198.5 0.0 copy-start.1
  198.5 2.2 copy-done.1
  200.7 23.4 %finish.1 = f32[56,8,128]{2,1,0:T(8,128)} custom-call(s32[1]{0:T(128)} %bitcast.8.row_ref, s32[28,8]{1,0:T(8,128)S(1)} %copy.9.pat_ref, f32[8,56,128]{2,1,0:T(8,128)S(1)} %get-tuple-element.17.grad_ref, f32[8192,128]{1,0:T(8,128)S(1)} %bitcast.18, f32[8192,128]{1,0:T(8,128)S(1)} %bitcast.19), custom_call_target="tpu_custom_call" | custom-call | flops 5000000000 | bytes 9000000 | tf_op jit(solution)/shard_map/finish/pallas_call | solution.py:631
Async XLA Ops:
  60.9 1.5 copy-start.2
  101.8 96.7 %copy-start = (f32[8,4,2,4,32,128]{5,4,3,2,1,0:T(8,128)S(1)}, f32[8,4,2,4,32,128]{5,4,3,2,1,0:T(8,128)}, u32[]{:S(2)}) copy-start(f32[8,4,2,4,32,128]{5,4,3,2,1,0:T(8,128)} %get-tuple-element.18) | copy-start | bytes 12582916
  198.5 2.2 copy-start.1

commit v4 on v3

--- a/solution.py
+++ b/solution.py
@@ -13,6 +13,9 @@
 F32 = jnp.float32
 BF16 = jnp.bfloat16
 MIB = 1 << 20
+TOGETHER = 4
+UNROLL = 8
+CHUNKS = 2
 
 
 def split_bf16(value):
@@ -27,12 +30,12 @@
     )
 
 
-def local_kernel(inv_tokens, core_ref, pat_ref, cot_ref, hid_ref, wgt_ref, proj_ref, back_ref, grad_ref, comp_ref, z_ref):
+def local_kernel(inv_tokens, core_ref, pat_ref, cot_ref, hid_ref, wgt_ref, proj_ref, back_ref, grad_ref, comp_ref, z_ref, w_ref):
     step = pl.program_id(0)
     core = core_ref[0]
-    slots = wgt_ref.shape[0]
+    _, slots, blk = wgt_ref.shape
     mine = slots // 2
-    blk = hid_ref.shape[1]
+    together = hid_ref.shape[1] // blk
     rank = proj_ref.shape[1]
     tokens = back_ref.shape[0]
     per_part = cot_ref.shape[2] // blk
@@ -49,29 +52,35 @@
         def _(i):
             z_ref[i] = jnp.zeros(z_ref.shape[1:], F32)
 
-    cols = [pat_ref[step, k] for k in range(slots)]
-    chosen = jnp.concatenate([cot_block(col, own) for col in cols], axis=1)
-    weight = jnp.concatenate([wgt_ref[k] for k in range(slots)], axis=1)
-    back = lax.dot_general(chosen, weight, (((1,), (1,)), ((), ())), preferred_element_type=F32)
-    back_ref[...] = back.astype(BF16)
-    hid = hid_ref[...]
-    wide = jnp.concatenate([cot_block(pat_ref[step, mine * core + j]) for j in range(mine)], axis=1)
-    grad = lax.dot_general(hid, wide, (((0,), (0,)), ((), ())), preferred_element_type=F32)
-    grad = grad * inv_tokens
-    for j in range(mine):
-        grad_ref[j] = grad[:, j * blk : (j + 1) * blk]
-    high, low = split_bf16(proj_ref[...])
-    both = jnp.dot(hid, jnp.concatenate([high, low], axis=1), preferred_element_type=F32)
-    y = both[:, :rank] + both[:, rank:]
-    for col in cols:
-
-        @pl.when(lax.rem(col, 2) == core)
-        def _(col=col):
-            z_ref[lax.div(col, 2)] += y
+    for b in range(together):
+        row = step * together + b
+        units = slice(b * blk, (b + 1) * blk)
+        cols = [pat_ref[row, k] for k in range(slots)]
+        chosen = jnp.concatenate([cot_block(col, own) for col in cols], axis=1)
+        w_ref[...] = wgt_ref[units].astype(F32).reshape(blk * slots, blk)
+        weight = jnp.concatenate(
+            [w_ref[pl.ds(k, blk, stride=slots), :].astype(BF16) for k in range(slots)], axis=1
+        )
+        back = lax.dot_general(chosen, weight, (((1,), (1,)), ((), ())), preferred_element_type=F32)
+        back_ref[:, units] = back.astype(BF16)
+        hid = hid_ref[:, units]
+        wide = jnp.concatenate([cot_block(pat_ref[row, mine * core + j]) for j in range(mine)], axis=1)
+        grad = lax.dot_general(hid, wide, (((0,), (0,)), ((), ())), preferred_element_type=F32)
+        grad = grad * inv_tokens
+        for j in range(mine):
+            grad_ref[j, units, :] = grad[:, j * blk : (j + 1) * blk]
+        high, low = split_bf16(proj_ref[units, :])
+        both = jnp.dot(hid, jnp.concatenate([high, low], axis=1), preferred_element_type=F32)
+        y = both[:, :rank] + both[:, rank:]
+        for col in cols:
+
+            @pl.when(lax.rem(col, 2) == core)
+            def _(col=col, y=y):
+                z_ref[lax.div(col, 2)] += y
 
     @pl.when(step == pl.num_programs(0) - 1)
     def _():
-        @pl.loop(0, half_blocks)
+        @pl.loop(0, half_blocks, unroll=UNROLL)
         def _(i):
             zh, zl = split_bf16(z_ref[i])
             out = lax.dot_general(
@@ -91,21 +100,22 @@
     rows = hidden.shape[1]
     rank = proj.shape[1]
     half_blocks = parts * part_cols // blk // 2
+    wide = TOGETHER * blk
     grid_spec = pltpu.PrefetchScalarGridSpec(
         num_scalar_prefetch=2,
-        grid=(block_rows,),
+        grid=(block_rows // TOGETHER,),
         in_specs=[
             pl.BlockSpec((parts, wide_tokens, part_cols), lambda r, *_: (0, 0, 0), pipeline_mode=pl.Buffered(1)),
-            pl.BlockSpec((wide_tokens, blk), lambda r, *_: (0, r)),
-            pl.BlockSpec((slots, blk, blk), lambda r, *_: (0, r, 0)),
-            pl.BlockSpec((blk, rank), lambda r, *_: (r, 0)),
+            pl.BlockSpec((wide_tokens, wide), lambda r, *_: (0, r)),
+            pl.BlockSpec((wide, slots, blk), lambda r, *_: (r, 0, 0)),
+            pl.BlockSpec((wide, rank), lambda r, *_: (r, 0)),
         ],
         out_specs=[
-            pl.BlockSpec((tokens, blk), lambda r, *_: (0, r)),
-            pl.BlockSpec((slots // 2, blk, blk), lambda r, *_: (0, r, 0)),
+            pl.BlockSpec((tokens, wide), lambda r, *_: (0, r)),
+            pl.BlockSpec((slots // 2, wide, blk), lambda r, *_: (0, r, 0)),
             pl.BlockSpec((half_blocks, blk, rank), lambda r, *_: (0, 0, 0), pipeline_mode=pl.Buffered(1)),
         ],
-        scratch_shapes=[pltpu.VMEM((half_blocks, wide_tokens, rank), F32)],
+        scratch_shapes=[pltpu.VMEM((half_blocks, wide_tokens, rank), F32), pltpu.VMEM((blk * slots, blk), F32)],
     )
     return pl.pallas_call(
         functools.partial(local_kernel, 1.0 / all_tokens),
@@ -115,7 +125,7 @@
             jax.ShapeDtypeStruct((slots // 2, rows, blk), F32),
             jax.ShapeDtypeStruct((half_blocks, blk, rank), F32),
         ),
-        compiler_params=pltpu.CompilerParams(vmem_limit_bytes=48 * MIB),
+        compiler_params=pltpu.CompilerParams(vmem_limit_bytes=56 * MIB),
         cost_estimate=pl.CostEstimate(flops=6_000_000_000, bytes_accessed=36_000_000, transcendentals=0),
         name="local_step",
     )(core, pattern, cot, hidden, weights, proj)
@@ -343,123 +353,186 @@
     send = wires.send
     zlow, zhigh = pl.ds(0, nz // 2), pl.ds(nz // 2, nz // 2)
 
+    chunk_rows = comp.shape[3] // CHUNKS
+    from_sib = []
+
+    class Chunk:
+        def __init__(self, index):
+            self.rows = pl.ds(index * chunk_rows, chunk_rows)
+
+        def start(self):
+            r = self.rows
+            self.far = (
+                send(xc.at[zlow, :, x2, r], cx.at[0, zlow, :, r], xp),
+                send(xc.at[zhigh, :, x2, r], cx.at[1, zhigh, :, r], xm),
+            )
+            self.near = [
+                send(xc.at[zhigh, :, x1, r], cx.at[2, zhigh, :, r], xp),
+                send(xc.at[zlow, :, x3, r], cx.at[3, zlow, :, r], xm),
+            ]
+
+        def middle(self):
+            r = self.rows
+            received(self.far[0])
+
+            @pl.loop(0, nz // 2)
+            def _(i):
+                xc[i, :, x1, r] = xc[i, :, x1, r] + cx[0, i, :, r]
+
+            self.near.append(send(xc.at[zlow, :, x1, r], cx.at[2, zlow, :, r], xp))
+            received(self.far[1])
+
+            @pl.loop(nz // 2, nz)
+            def _(i):
+                xc[i, :, x3, r] = xc[i, :, x3, r] + cx[1, i, :, r]
+
+            self.near.append(send(xc.at[zhigh, :, x3, r], cx.at[3, zhigh, :, r], xm))
+
+        def along_y(self):
+            r = self.rows
+            received(*self.near)
+
+            @pl.loop(0, nz)
+            def _(i):
+                xc[i, :, x, r] = xc[i, :, x, r] + cx[2, i, :, r] + cx[3, i, :, r]
+
+            self.moved = [
+                send(xc.at[:, here.shift("y", j), x, r], cy.at[j - 1, :, r], here.device("y", j)) for j in range(1, ny)
+            ]
+
+        def along_z(self):
+            r = self.rows
+            received(*self.moved)
+
+            @pl.loop(0, nz)
+            def _(i):
+                xc[i, y, x, r] = xc[i, y, x, r] + (cy[0, i, r] + cy[1, i, r] + cy[2, i, r])
+
+            self.moved = [
+                send(xc.at[here.shift("z", j), y, x, r], cz.at[j - 1, r], here.device("z", j)) for j in range(1, nz)
+            ]
+
+        def total(self):
+            r = self.rows
+            received(*self.moved)
+            total = xc[z, y, x, r]
+            for j in range(nz - 1):
+                total = total + cz[j, r]
+            comp_o[z, y, c, x, r] = total
+            mine = comp_o.at[z, y, c, x, r]
+            self.moved = [send(mine, mine, here.device("z", j)) for j in range(1, nz)]
+
+        def back_y(self):
+            received(*self.moved)
+            column = comp_o.at[:, y, c, x, self.rows]
+            self.moved = [send(column, column, here.device("y", j)) for j in range(1, ny)]
+
+        def copy_to(self, layers, at, device):
+            part = comp_o.at[layers, :, c, at, self.rows]
+            return send(part, part, device)
+
+        def back_x(self):
+            received(*self.moved)
+            every = slice(None)
+            self.moved = [self.copy_to(every, x, xp), self.copy_to(every, x, xm)]
+            from_sib.append(self.copy_to(every, x, sib))
+
+        def back_far(self):
+            every = slice(None)
+            received(self.moved[0])
+            far = [self.copy_to(zlow, x3, xp)]
+            received(self.moved[1])
+            far.append(self.copy_to(zhigh, x1, xm))
+            self.moved = far
+            for at in (x3, x1):
+                from_sib.append(self.copy_to(every, at, sib))
+
+        def finish(self):
+            for copy, layers in zip(self.moved, (zlow, zhigh)):
+                received(copy)
+                from_sib.append(self.copy_to(layers, x2, sib))
+
     keep_comp.wait()
-    c_far = (
-        send(xc.at[zlow, :, x2], cx.at[0, zlow], xp),
-        send(xc.at[zhigh, :, x2], cx.at[1, zhigh], xm),
-    )
-    c_near = [
-        send(xc.at[zhigh, :, x1], cx.at[2, zhigh], xp),
-        send(xc.at[zlow, :, x3], cx.at[3, zlow], xm),
-    ]
+    first, second = Chunk(0), Chunk(1)
+    first.start()
     keep_grad.wait()
     a_far = (send(xg.at[0, :, y2], ya.at[0], yp), send(xg.at[1, :, y2], ya.at[1], ym))
     b_dist = nz // 2
 
-    def b_send(slot_at, dist):
-        first = slot_at == "far"
-        plus = here.shift("z", dist)
-        minus = here.shift("z", -dist)
-        if first:
+    def ring_send(source, arrived, slots, dist):
+        plus, minus = here.shift("z", dist), here.shift("z", -dist)
+        if dist == b_dist:
             return (
-                [send(xg.at[2, plus], zb.at[0, dist - 1, 0], zp)],
-                [send(xg.at[3, minus], zb.at[1, dist - 1, 1], zm)],
+                send(source(slots[0], plus), arrived.at[0, dist - 1, 0], zp),
+                send(source(slots[1], minus), arrived.at[1, dist - 1, 1], zm),
             )
+        both = pl.ds(slots[0], 2)
         return (
-            [send(xg.at[pl.ds(2, 2), plus], zb.at[0, dist - 1], zp)],
-            [send(xg.at[pl.ds(2, 2), minus], zb.at[1, dist - 1], zm)],
+            send(source(both, plus), arrived.at[0, dist - 1], zp),
+            send(source(both, minus), arrived.at[1, dist - 1], zm),
         )
 
-    b_moving = b_send("far", b_dist)
+    def b_send(dist):
+        return ring_send(lambda s, layer: xg.at[s, layer], zb, (2, 3), dist)
+
+    def a_send(dist):
+        return ring_send(lambda s, layer: xg.at[s, layer, y], za, (0, 1), dist)
+
+    def arrived_slots(dist, side):
+        return (side,) if dist == b_dist else (0, 1)
+
+    def b_step(dist, moving):
+        for side in (0, 1):
+            received(moving[side])
+            layer = here.shift("z", (dist - 1) * (1 - 2 * side))
+            for s in arrived_slots(dist, side):
+                add_into(xg, [2 + s, layer, None], zb.at[side, dist - 1, s], ny)
+        return b_send(dist - 1) if dist > 1 else None
+
+    def a_step(dist, moving):
+        for side in (0, 1):
+            received(moving[side])
+            layer = here.shift("z", (dist - 1) * (1 - 2 * side))
+            for s in arrived_slots(dist, side):
+                xg[s, layer, y] = xg[s, layer, y] + za[side, dist - 1, s]
+        return a_send(dist - 1) if dist > 1 else None
+
+    b_moving = b_send(b_dist)
     a_near = [send(xg.at[1, :, y1], ya.at[2], yp), send(xg.at[0, :, y3], ya.at[3], ym)]
-
-    def b_step(dist, moving):
-        for side, slots in ((0, (0,) if dist == b_dist else (0, 1)), (1, (1,) if dist == b_dist else (0, 1))):
-            received(*moving[side])
-            layer = here.shift("z", (dist - 1) * (1 - 2 * side))
-            for s in slots:
-                add_into(xg, [2 + s, layer, None], zb.at[side, dist - 1, s], ny)
-        return b_send("near", dist - 1) if dist > 1 else None
-
+    first.middle()
+    second.start()
     b_moving = b_step(b_dist, b_moving)
-    received(c_far[0])
-    add_into(xc, [None, slice(None), x1], cx.at[0], nz // 2)
-    c_near.append(send(xc.at[zlow, :, x1], cx.at[2, zlow], xp))
-    received(c_far[1])
-
-    @pl.loop(nz // 2, nz)
-    def _(i):
-        xc[i, :, x3] = xc[i, :, x3] + cx[1, i]
-
-    c_near.append(send(xc.at[zhigh, :, x3], cx.at[3, zhigh], xm))
+    second.middle()
     received(a_far[0])
     add_into(xg, [0, None, y1], ya.at[0], nz)
     a_near.append(send(xg.at[0, :, y1], ya.at[4], yp))
     received(a_far[1])
     add_into(xg, [1, None, y3], ya.at[1], nz)
     a_near.append(send(xg.at[1, :, y3], ya.at[5], ym))
+    first.along_y()
     b_moving = b_step(3, b_moving)
-
-    received(*c_near)
+    first.along_z()
+    second.along_y()
+    first.total()
+    second.along_z()
+    first.back_y()
+    b_moving = b_step(2, b_moving)
+    second.total()
+    first.back_x()
+    second.back_y()
+    received(*a_near)
 
     @pl.loop(0, nz)
     def _(i):
-        xc[i, :, x] = xc[i, :, x] + cx[2, i] + cx[3, i]
-
-    c_y = [send(xc.at[:, here.shift("y", j), x], cy.at[j - 1], here.device("y", j)) for j in range(1, ny)]
-    received(*c_y)
-
-    @pl.loop(0, nz)
-    def _(i):
-        xc[i, y, x] = xc[i, y, x] + (cy[0, i] + cy[1, i] + cy[2, i])
-
-    c_z = [send(xc.at[here.shift("z", j), y, x], cz.at[j - 1], here.device("z", j)) for j in range(1, nz)]
-    b_moving = b_step(2, b_moving)
-    received(*c_z)
-    total = xc[z, y, x]
-    for j in range(nz - 1):
-        total = total + cz[j]
-    comp_o[z, y, c, x] = total
-    mine = comp_o.at[z, y, c, x]
-    g_z = [send(mine, mine, here.device("z", j)) for j in range(1, nz)]
-    received(*a_near)
-
-    @pl.loop(0, nz)
-    def _(i):
-        xg[0, i, y] = xg[0, i, y] + ya[2 + 2, i] + ya[3, i]
+        xg[0, i, y] = xg[0, i, y] + ya[4, i] + ya[3, i]
         xg[1, i, y] = xg[1, i, y] + ya[2, i] + ya[5, i]
 
-    def a_send(dist):
-        plus, minus = here.shift("z", dist), here.shift("z", -dist)
-        if dist == b_dist:
-            return (
-                [send(xg.at[0, plus, y], za.at[0, dist - 1, 0], zp)],
-                [send(xg.at[1, minus, y], za.at[1, dist - 1, 1], zm)],
-            )
-        return (
-            [send(xg.at[pl.ds(0, 2), plus, y], za.at[0, dist - 1], zp)],
-            [send(xg.at[pl.ds(0, 2), minus, y], za.at[1, dist - 1], zm)],
-        )
-
-    def a_step(dist, moving):
-        for side, slots in ((0, (0,) if dist == b_dist else (0, 1)), (1, (1,) if dist == b_dist else (0, 1))):
-            received(*moving[side])
-            layer = here.shift("z", (dist - 1) * (1 - 2 * side))
-            for s in slots:
-                xg[s, layer, y] = xg[s, layer, y] + za[side, dist - 1, s]
-        return a_send(dist - 1) if dist > 1 else None
-
     a_moving = a_send(b_dist)
-    received(*g_z)
-    column = comp_o.at[:, y, c, x]
-    g_y = [send(column, column, here.device("y", j)) for j in range(1, ny)]
+    second.back_x()
     b_step(1, b_moving)
     b2_far = (send(xg.at[2, z, y2], yb.at[0], yp), send(xg.at[3, z, y2], yb.at[1], ym))
     b2_near = [send(xg.at[3, z, y1], yb.at[2], yp), send(xg.at[2, z, y3], yb.at[3], ym)]
-    received(*g_y)
-    plane = comp_o.at[:, :, c, x]
-    g_x = (send(plane, plane, xp), send(plane, plane, xm))
-    from_sib = [send(plane, plane, sib)]
+    first.back_far()
     a_moving = a_step(b_dist, a_moving)
     received(b2_far[0])
     xg[2, z, y1] = xg[2, z, y1] + yb[0]
@@ -468,7 +541,9 @@
     xg[3, z, y3] = xg[3, z, y3] + yb[1]
     b2_near.append(send(xg.at[3, z, y3], yb.at[5], ym))
     a_moving = a_step(3, a_moving)
+    second.back_far()
     a_moving = a_step(2, a_moving)
+    first.finish()
     received(*b2_near)
     xg[2, z, y] = xg[2, z, y] + yb[4] + yb[3]
     xg[3, z, y] = xg[3, z, y] + yb[2] + yb[5]
@@ -478,21 +553,7 @@
     swap = send(xg.at[:, z, y, theirs], grad_o.at[pl.ds(c * 4, 4)], sib)
     for s in range(4):
         grad_o[c * 4 + s] = xg[s, z, y, pl.ds(pl.multiple_of(c * units, 8), units)]
-    received(g_x[0])
-    part = comp_o.at[zlow, :, c, x3]
-    far = [send(part, part, xp)]
-    received(g_x[1])
-    part = comp_o.at[zhigh, :, c, x1]
-    far.append(send(part, part, xm))
-    for at in (x3, x1):
-        part = comp_o.at[:, :, c, at]
-        from_sib.append(send(part, part, sib))
-    received(far[0])
-    part = comp_o.at[zlow, :, c, x2]
-    from_sib.append(send(part, part, sib))
-    received(far[1])
-    part = comp_o.at[zhigh, :, c, x2]
-    from_sib.append(send(part, part, sib))
+    second.finish()
     received(swap, *from_sib)
     wires.drain()
 
@@ -502,7 +563,7 @@
     piece = comp.shape[3:]
     any_spec = pl.BlockSpec(memory_space=pl.ANY)
     vmem = pl.BlockSpec(memory_space=pltpu.VMEM)
-    copies = 96
+    copies = 112
     return pl.pallas_call(
         functools.partial(reduce_kernel, ny, nz, nx),
         in_specs=[any_spec] * 2,
@@ -660,7 +721,7 @@
     cot = cot.reshape(nx, -1, cotangent.shape[1])
     hid = hid.reshape(-1, hidden.shape[1])
     input_grad, grad, comp = local_step(
-        core, pattern, cot, hid, weights.transpose(1, 0, 2), proj.reshape(-1, rank), all_tokens
+        core, pattern, cot, hid, weights, proj.reshape(-1, rank), all_tokens
     )
     grad, comp = reduce_all(
         ny, nz, nx, grad.reshape(slots // 2, nz, ny, 2 * dev_rows, blk), comp.reshape(nz, ny, nx, -1, rank)

time: 225 us -> 201 us (0.89)
  Pallas kernels: 212 us -> 195 us
  local copies, waits for them, and re-layouts: 11.5 us -> 5.15 us
    pallas_call x1, Pallas kernels: 39.4 us -> 30.8 us  [local_step(): pl.pallas_call(functools.partial(local_kernel, 1.0 / all_tokens), grid_sp...]
    pallas_call x1, Pallas kernels: 96.7 us -> 88.4 us  [reduce_all(): pl.pallas_call(functools.partial(reduce_kernel, ny, nz, nx), in_specs=[an...]
    unnamed x8 -> x9, local copies, waits for them, and re-layouts: 11.5 us -> 5.15 us
where the time goes in v4:
time: 201 us
  Pallas kernels  195 us (97%)
  local copies, waits for them, and re-layouts  5.15 us (3%)
    pallas_call x1, Pallas kernels, reduce_all(): pl.pallas_call(functools.partial(reduce_kernel, ny, nz, nx), in_specs=[an...  88.4 us
    pallas_call x1, Pallas kernels, gather(): pl.pallas_call(functools.partial(gather_kernel, ny, nz, nx), in_specs=[an...  52.4 us
    pallas_call x1, Pallas kernels, local_step(): pl.pallas_call(functools.partial(local_kernel, 1.0 / all_tokens), grid_sp...  30.8 us
    pallas_call x1, Pallas kernels, finish(): pl.pallas_call(finish_kernel, in_specs=[smem, smem, vmem, vmem, vmem], ou...  23.6 us
    unnamed x9, local copies, waits for them, and re-layouts  5.15 us

profile of v4, /device:TPU:1, one launch (start us, length us, event | category | flops | bytes accessed | tf_op | source)
XLA Modules:
  0.0 201.0 jit_solution(5714606892332815258)
XLA Ops:
  0.6 1.4 copy.8.pat_ref
  2.0 52.4 %gather.1 = (bf16[4,2,256,2048]{3,2,1,0:T(8,128)(2,1)}, bf16[2,256,3584]{2,1,0:T(8,128)(2,1)}, f32[8,4,2,56,128]{4,3,2,1,0:T(8,128)}, f32[8,4,2,4,32,128]{5,4,3,2,1,0:T(8,128)}) custom-call(bf16[256,2048]{1,0:T(8,128)(2,1)} %cot.1, bf16[256,3584]{1,0:T(8,128)(2,1)} %hid.1, f32[56,128]{1,0:T(8,128)} %bitcast.18, f32[32,128]{1,0:T(8,128)} %bitcast.19), custom_call_target="tpu_custom_call" | custom-call | bytes 60000000 | tf_op jit(solution)/shard_map/gather/pallas_call | solution.py:302
  54.4 30.8 %local_step.1 = (bf16[256,3584]{1,0:T(8,128)(2,1)}, f32[4,3584,128]{2,1,0:T(8,128)}, f32[32,128,128]{2,1,0:T(8,128)}) custom-call(s32[1]{0:T(128)} %bitcast.core_ref, s32[28,8]{1,0:T(8,128)} %copy.8.pat_ref, bf16[4,512,2048]{2,1,0:T(8,128)(2,1)} %bitcast.20, bf16[512,3584]{1,0:T(8,128)(2,1)} %bitcast.21, bf16[3584,8,128]{2,1,0:T(8,128)(2,1)} %wgt_ref.1, ...), custom_call_target="tpu_custom_call" | custom-call | flops 6000000000 | bytes 36000000 | tf_op jit(solution)/shard_map/local_step/pallas_call | solution.py:120
  85.2 0.0 copy-start
  85.2 1.6 copy-done
  86.8 0.0 copy-start.1
  86.8 0.0 copy-start.2
  86.8 88.4 %reduce.1 = (f32[8,56,128]{2,1,0:T(8,128)S(1)}, f32[8,4,2,4,32,128]{5,4,3,2,1,0:T(8,128)}) custom-call(f32[4,8,4,112,128]{4,3,2,1,0:T(8,128)} %bitcast.17, f32[8,4,4,32,128]{4,3,2,1,0:T(8,128)S(1)} %bitcast.14), custom_call_target="tpu_custom_call" | custom-call | bytes 100000000 | tf_op jit(solution)/shard_map/reduce/pallas_call | solution.py:567
  175.2 0.0 copy-done.1
  175.2 0.0 copy-done.2
  175.2 0.0 copy-start.3
  175.2 2.2 %copy-done.3 = f32[8,4,2,4,32,128]{5,4,3,2,1,0:T(8,128)S(1)} copy-done((f32[8,4,2,4,32,128]{5,4,3,2,1,0:T(8,128)S(1)}, f32[8,4,2,4,32,128]{5,4,3,2,1,0:T(8,128)}, u32[]{:S(2)}) %copy-start.3) | copy-done | bytes 4194328
  177.4 23.6 %finish.1 = f32[56,8,128]{2,1,0:T(8,128)} custom-call(s32[1]{0:T(128)} %bitcast.7.row_ref, s32[28,8]{1,0:T(8,128)S(1)} %copy-done.1, f32[8,56,128]{2,1,0:T(8,128)S(1)} %get-tuple-element.17.grad_ref, f32[8192,128]{1,0:T(8,128)S(1)} %bitcast.15, f32[8192,128]{1,0:T(8,128)S(1)} %bitcast.16), custom_call_target="tpu_custom_call" | custom-call | flops 5000000000 | bytes 9000000 | tf_op jit(solution)/shard_map/finish/pallas_call | solution.py:692
Async XLA Ops:
  85.2 1.6 copy-start
  86.8 88.4 %copy-start.1 = (s32[28,8]{1,0:T(8,128)S(1)}, s32[28,8]{1,0:T(8,128)}, u32[]{:S(2)}) copy-start(s32[28,8]{1,0:T(8,128)} %copy.8.pat_ref) | copy-start | bytes 2692
  86.8 88.4 %copy-start.2 = (f32[8,4,2,4,32,128]{5,4,3,2,1,0:T(8,128)S(1)}, f32[8,4,2,4,32,128]{5,4,3,2,1,0:T(8,128)}, u32[]{:S(2)}) copy-start(f32[8,4,2,4,32,128]{5,4,3,2,1,0:T(8,128)} %get-tuple-element.18) | copy-start | bytes 12582916
  175.2 2.2 %copy-start.3 = (f32[8,4,2,4,32,128]{5,4,3,2,1,0:T(8,128)S(1)}, f32[8,4,2,4,32,128]{5,4,3,2,1,0:T(8,128)}, u32[]{:S(2)}) copy-start(f32[8,4,2,4,32,128]{5,4,3,2,1,0:T(8,128)} %get-tuple-element.19) | copy-start | bytes 12582916

commit v5 on v4

--- a/solution.py
+++ b/solution.py
@@ -340,7 +340,7 @@
     x, y, z, c = (here.at[name] for name in "xyzc")
     wires = Wires(send_sems, recv_sems, local_sems)
     keep_comp = wires.keep(comp, xc)
-    keep_grad = wires.keep(grad, xg)
+    keep_grad = [wires.keep(grad.at[s], xg.at[s]) for s in (2, 3, 0, 1)]
     sib = here.device("c", 1)
     partners = [here.device("x", j) for j in range(1, nx)] + [here.device("y", j) for j in range(1, ny)]
     partners += [here.device("z", j) for j in range(1, nz)] + [sib]
@@ -455,53 +455,58 @@
     keep_comp.wait()
     first, second = Chunk(0), Chunk(1)
     first.start()
-    keep_grad.wait()
+    class Ring:
+        def __init__(self, source, arrived, side, index, add, dist):
+            self.source, self.arrived, self.side, self.index, self.add = source, arrived, side, index, add
+            self.send(dist)
+
+        def layer(self, dist):
+            return here.shift("z", dist if self.side == 0 else -dist)
+
+        def send(self, dist):
+            self.dist = dist
+            target = self.arrived.at[self.side, dist - 1, self.index]
+            self.copy = send(self.source(self.index, self.layer(dist)), target, (zp, zm)[self.side])
+
+        def step(self):
+            if self.dist == 0:
+                return
+            received(self.copy)
+            self.add(self.index, self.layer(self.dist - 1), self.side, self.dist - 1)
+            if self.dist > 1:
+                self.send(self.dist - 1)
+            else:
+                self.dist = 0
+
+    far_z = nz // 2
+
+    def b_add(index, layer, side, slot_at):
+        add_into(xg, [2 + index, layer, None], zb.at[side, slot_at, index], ny)
+
+    def a_add(index, layer, side, slot_at):
+        xg[index, layer, y] = xg[index, layer, y] + za[side, slot_at, index]
+
+    def b_ring(side, index, dist):
+        return Ring(lambda s, layer: xg.at[2 + s, layer], zb, side, index, b_add, dist)
+
+    def a_ring(side, index, dist):
+        return Ring(lambda s, layer: xg.at[s, layer, y], za, side, index, a_add, dist)
+
+    keep_grad[0].wait()
+    keep_grad[1].wait()
+    b_rings = [b_ring(0, 0, far_z), b_ring(1, 1, far_z), b_ring(0, 1, far_z - 1), b_ring(1, 0, far_z - 1)]
+    keep_grad[2].wait()
+    keep_grad[3].wait()
     a_far = (send(xg.at[0, :, y2], ya.at[0], yp), send(xg.at[1, :, y2], ya.at[1], ym))
-    b_dist = nz // 2
-
-    def ring_send(source, arrived, slots, dist):
-        plus, minus = here.shift("z", dist), here.shift("z", -dist)
-        if dist == b_dist:
-            return (
-                send(source(slots[0], plus), arrived.at[0, dist - 1, 0], zp),
-                send(source(slots[1], minus), arrived.at[1, dist - 1, 1], zm),
-            )
-        both = pl.ds(slots[0], 2)
-        return (
-            send(source(both, plus), arrived.at[0, dist - 1], zp),
-            send(source(both, minus), arrived.at[1, dist - 1], zm),
-        )
-
-    def b_send(dist):
-        return ring_send(lambda s, layer: xg.at[s, layer], zb, (2, 3), dist)
-
-    def a_send(dist):
-        return ring_send(lambda s, layer: xg.at[s, layer, y], za, (0, 1), dist)
-
-    def arrived_slots(dist, side):
-        return (side,) if dist == b_dist else (0, 1)
-
-    def b_step(dist, moving):
-        for side in (0, 1):
-            received(moving[side])
-            layer = here.shift("z", (dist - 1) * (1 - 2 * side))
-            for s in arrived_slots(dist, side):
-                add_into(xg, [2 + s, layer, None], zb.at[side, dist - 1, s], ny)
-        return b_send(dist - 1) if dist > 1 else None
-
-    def a_step(dist, moving):
-        for side in (0, 1):
-            received(moving[side])
-            layer = here.shift("z", (dist - 1) * (1 - 2 * side))
-            for s in arrived_slots(dist, side):
-                xg[s, layer, y] = xg[s, layer, y] + za[side, dist - 1, s]
-        return a_send(dist - 1) if dist > 1 else None
-
-    b_moving = b_send(b_dist)
     a_near = [send(xg.at[1, :, y1], ya.at[2], yp), send(xg.at[0, :, y3], ya.at[3], ym)]
+
+    def advance(rings):
+        for ring in rings:
+            ring.step()
+
     first.middle()
     second.start()
-    b_moving = b_step(b_dist, b_moving)
+    advance(b_rings[:2])
     second.middle()
     received(a_far[0])
     add_into(xg, [0, None, y1], ya.at[0], nz)
@@ -509,45 +514,54 @@
     received(a_far[1])
     add_into(xg, [1, None, y3], ya.at[1], nz)
     a_near.append(send(xg.at[1, :, y3], ya.at[5], ym))
+    advance(b_rings[2:])
     first.along_y()
-    b_moving = b_step(3, b_moving)
+    advance(b_rings[:2])
     first.along_z()
     second.along_y()
+    advance(b_rings[2:])
     first.total()
     second.along_z()
+    advance(b_rings[:2])
     first.back_y()
-    b_moving = b_step(2, b_moving)
     second.total()
+    advance(b_rings[2:])
     first.back_x()
     second.back_y()
-    received(*a_near)
+    received(a_near[2], a_near[1])
 
     @pl.loop(0, nz)
     def _(i):
         xg[0, i, y] = xg[0, i, y] + ya[4, i] + ya[3, i]
+
+    a_rings = [a_ring(0, 0, far_z), None, None, a_ring(1, 0, far_z - 1)]
+    received(a_near[0], a_near[3])
+
+    @pl.loop(0, nz)
+    def _(i):
         xg[1, i, y] = xg[1, i, y] + ya[2, i] + ya[5, i]
 
-    a_moving = a_send(b_dist)
+    a_rings[1:3] = [a_ring(1, 1, far_z), a_ring(0, 1, far_z - 1)]
     second.back_x()
-    b_step(1, b_moving)
+    advance(b_rings[:2])
     b2_far = (send(xg.at[2, z, y2], yb.at[0], yp), send(xg.at[3, z, y2], yb.at[1], ym))
     b2_near = [send(xg.at[3, z, y1], yb.at[2], yp), send(xg.at[2, z, y3], yb.at[3], ym)]
     first.back_far()
-    a_moving = a_step(b_dist, a_moving)
+    advance(a_rings)
     received(b2_far[0])
     xg[2, z, y1] = xg[2, z, y1] + yb[0]
     b2_near.append(send(xg.at[2, z, y1], yb.at[4], yp))
     received(b2_far[1])
     xg[3, z, y3] = xg[3, z, y3] + yb[1]
     b2_near.append(send(xg.at[3, z, y3], yb.at[5], ym))
-    a_moving = a_step(3, a_moving)
+    advance(a_rings)
     second.back_far()
-    a_moving = a_step(2, a_moving)
+    advance(a_rings)
     first.finish()
     received(*b2_near)
     xg[2, z, y] = xg[2, z, y] + yb[4] + yb[3]
     xg[3, z, y] = xg[3, z, y] + yb[2] + yb[5]
-    a_step(1, a_moving)
+    advance(a_rings)
     units = grad_o.shape[1]
     theirs = pl.ds(pl.multiple_of((1 - c) * units, 8), units)
     swap = send(xg.at[:, z, y, theirs], grad_o.at[pl.ds(c * 4, 4)], sib)
@@ -563,7 +577,7 @@
     piece = comp.shape[3:]
     any_spec = pl.BlockSpec(memory_space=pl.ANY)
     vmem = pl.BlockSpec(memory_space=pltpu.VMEM)
-    copies = 112
+    copies = 128
     return pl.pallas_call(
         functools.partial(reduce_kernel, ny, nz, nx),
         in_specs=[any_spec] * 2,
@@ -584,7 +598,7 @@
             pltpu.VMEM((nz - 1,) + piece, F32),
             pltpu.SemaphoreType.DMA((copies,)),
             pltpu.SemaphoreType.DMA((copies,)),
-            pltpu.SemaphoreType.DMA((2,)),
+            pltpu.SemaphoreType.DMA((5,)),
         ],
         compiler_params=pltpu.CompilerParams(
             collective_id=2, has_side_effects=True, vmem_limit_bytes=48 * MIB

time: 201 us -> 195 us (0.970)
  Pallas kernels: 195 us -> 189 us
    pallas_call x1, Pallas kernels: 88.4 us -> 81.9 us  [reduce_all(): pl.pallas_call(functools.partial(reduce_kernel, ny, nz, nx), in_specs=[an...]
where the time goes in v5:
time: 195 us
  Pallas kernels  189 us (97%)
  local copies, waits for them, and re-layouts  5.15 us (3%)
    pallas_call x1, Pallas kernels, reduce_all(): pl.pallas_call(functools.partial(reduce_kernel, ny, nz, nx), in_specs=[an...  81.9 us
    pallas_call x1, Pallas kernels, gather(): pl.pallas_call(functools.partial(gather_kernel, ny, nz, nx), in_specs=[an...  52.4 us
    pallas_call x1, Pallas kernels, local_step(): pl.pallas_call(functools.partial(local_kernel, 1.0 / all_tokens), grid_sp...  31.1 us
    pallas_call x1, Pallas kernels, finish(): pl.pallas_call(finish_kernel, in_specs=[smem, smem, vmem, vmem, vmem], ou...  23.6 us
    unnamed x9, local copies, waits for them, and re-layouts  5.15 us

profile of v5, /device:TPU:1, one launch (start us, length us, event | category | flops | bytes accessed | tf_op | source)
XLA Modules:
  0.0 194.9 jit_solution(9190549337153798846)
XLA Ops:
  0.6 1.4 copy.8.pat_ref
  2.0 52.4 %gather.1 = (bf16[4,2,256,2048]{3,2,1,0:T(8,128)(2,1)}, bf16[2,256,3584]{2,1,0:T(8,128)(2,1)}, f32[8,4,2,56,128]{4,3,2,1,0:T(8,128)}, f32[8,4,2,4,32,128]{5,4,3,2,1,0:T(8,128)}) custom-call(bf16[256,2048]{1,0:T(8,128)(2,1)} %cot.1, bf16[256,3584]{1,0:T(8,128)(2,1)} %hid.1, f32[56,128]{1,0:T(8,128)} %bitcast.18, f32[32,128]{1,0:T(8,128)} %bitcast.19), custom_call_target="tpu_custom_call" | custom-call | bytes 60000000 | tf_op jit(solution)/shard_map/gather/pallas_call | solution.py:302
  54.4 31.1 %local_step.1 = (bf16[256,3584]{1,0:T(8,128)(2,1)}, f32[4,3584,128]{2,1,0:T(8,128)}, f32[32,128,128]{2,1,0:T(8,128)}) custom-call(s32[1]{0:T(128)} %bitcast.core_ref, s32[28,8]{1,0:T(8,128)} %copy.8.pat_ref, bf16[4,512,2048]{2,1,0:T(8,128)(2,1)} %bitcast.20, bf16[512,3584]{1,0:T(8,128)(2,1)} %bitcast.21, bf16[3584,8,128]{2,1,0:T(8,128)(2,1)} %wgt_ref.1, ...), custom_call_target="tpu_custom_call" | custom-call | flops 6000000000 | bytes 36000000 | tf_op jit(solution)/shard_map/local_step/pallas_call | solution.py:120
  85.6 0.0 copy-start
  85.6 1.6 copy-done
  87.2 0.0 copy-start.1
  87.2 0.0 copy-start.2
  87.2 81.9 %reduce.1 = (f32[8,56,128]{2,1,0:T(8,128)S(1)}, f32[8,4,2,4,32,128]{5,4,3,2,1,0:T(8,128)}) custom-call(f32[4,8,4,112,128]{4,3,2,1,0:T(8,128)} %bitcast.17, f32[8,4,4,32,128]{4,3,2,1,0:T(8,128)S(1)} %bitcast.14), custom_call_target="tpu_custom_call" | custom-call | bytes 100000000 | tf_op jit(solution)/shard_map/reduce/pallas_call | solution.py:581
  169.0 0.0 copy-done.1
  169.1 0.0 copy-done.2
  169.1 0.0 copy-start.3
  169.1 2.2 %copy-done.3 = f32[8,4,2,4,32,128]{5,4,3,2,1,0:T(8,128)S(1)} copy-done((f32[8,4,2,4,32,128]{5,4,3,2,1,0:T(8,128)S(1)}, f32[8,4,2,4,32,128]{5,4,3,2,1,0:T(8,128)}, u32[]{:S(2)}) %copy-start.3) | copy-done | bytes 4194328
  171.3 23.6 %finish.1 = f32[56,8,128]{2,1,0:T(8,128)} custom-call(s32[1]{0:T(128)} %bitcast.7.row_ref, s32[28,8]{1,0:T(8,128)S(1)} %copy-done.1, f32[8,56,128]{2,1,0:T(8,128)S(1)} %get-tuple-element.17.grad_ref, f32[8192,128]{1,0:T(8,128)S(1)} %bitcast.15, f32[8192,128]{1,0:T(8,128)S(1)} %bitcast.16), custom_call_target="tpu_custom_call" | custom-call | flops 5000000000 | bytes 9000000 | tf_op jit(solution)/shard_map/finish/pallas_call | solution.py:706
Async XLA Ops:
  85.6 1.6 copy-start
  87.2 81.9 %copy-start.1 = (s32[28,8]{1,0:T(8,128)S(1)}, s32[28,8]{1,0:T(8,128)}, u32[]{:S(2)}) copy-start(s32[28,8]{1,0:T(8,128)} %copy.8.pat_ref) | copy-start | bytes 2692
  87.2 81.9 %copy-start.2 = (f32[8,4,2,4,32,128]{5,4,3,2,1,0:T(8,128)S(1)}, f32[8,4,2,4,32,128]{5,4,3,2,1,0:T(8,128)}, u32[]{:S(2)}) copy-start(f32[8,4,2,4,32,128]{5,4,3,2,1,0:T(8,128)} %get-tuple-element.18) | copy-start | bytes 12582916
  169.1 2.2 %copy-start.3 = (f32[8,4,2,4,32,128]{5,4,3,2,1,0:T(8,128)S(1)}, f32[8,4,2,4,32,128]{5,4,3,2,1,0:T(8,128)}, u32[]{:S(2)}) copy-start(f32[8,4,2,4,32,128]{5,4,3,2,1,0:T(8,128)} %get-tuple-element.19) | copy-start | bytes 12582916

commit v6 on v5

--- a/solution.py
+++ b/solution.py
@@ -618,22 +618,18 @@
     return exact_dot(left, right, ((1,), (0,)))
 
 
-def spd_inverse(mat, eye):
-    n = mat.shape[0]
-    bound = jnp.max(jnp.sum(jnp.abs(mat), axis=1, keepdims=True))
-    start = eye * (2.0 / (bound + math.sqrt(EPS)))
-
+def spd_inverse(mat, start, eye):
     def unfinished(state):
         count, previous, residual, _ = state
-        return (count < 100) & (residual > 2e-6) & ((residual < 0.5 * previous) | (residual > 0.1))
+        return (count < 100) & (residual > 1e-5) & ((residual < 0.5 * previous) | (residual > 0.1))
 
     def body(state):
         count, _, residual, guess = state
         gap = eye - mul(mat, guess)
         guess = guess + mul(guess, gap)
-        return count + 1, residual, jnp.max(jnp.abs(gap)), guess
-
-    state = lax.while_loop(unfinished, body, (0, jnp.float32(4.0), jnp.float32(2.0), start))
+        return count + 1, residual, jnp.sqrt(jnp.sum(gap * gap)), guess
+
+    state = lax.while_loop(unfinished, body, (0, jnp.float32(64.0), jnp.float32(32.0), start))
     return state[3]
 
 
@@ -652,7 +648,11 @@
         root = mul(root, middle)
         inverse = mul(middle, inverse)
     half = 0.5 * jnp.sqrt(frob) * (root + root.T) + math.sqrt(EPS) * eye
-    half_inv = spd_inverse(half, eye)
+    near = inverse / jnp.sqrt(frob)
+    norm = jnp.max(jnp.sum(jnp.abs(near), axis=1, keepdims=True))
+    shift = math.sqrt(EPS)
+    start = near * (1.0 / (1.0 + 0.5 * jnp.minimum(shift * norm, 1.0)))
+    half_inv = spd_inverse(half, start, eye)
     return -mul(inverse, half_inv) / (math.sqrt(EPS) * jnp.sqrt(frob))
 
 

time: 195 us -> 193 us (0.990)
  Pallas kernels: 189 us -> 187 us
    pallas_call x1, Pallas kernels: 23.6 us -> 21.3 us  [finish(): pl.pallas_call(finish_kernel, in_specs=[smem, smem, vmem, vmem, vmem], ou...]
where the time goes in v6:
time: 193 us; the launch traced here: 192 us
  Pallas kernels  187 us (97%)
  local copies, waits for them, and re-layouts  5.15 us (3%)
    pallas_call x1, Pallas kernels, reduce_all(): pl.pallas_call(functools.partial(reduce_kernel, ny, nz, nx), in_specs=[an...  82 us
    pallas_call x1, Pallas kernels, gather(): pl.pallas_call(functools.partial(gather_kernel, ny, nz, nx), in_specs=[an...  52.4 us
    pallas_call x1, Pallas kernels, local_step(): pl.pallas_call(functools.partial(local_kernel, 1.0 / all_tokens), grid_sp...  30.9 us
    pallas_call x1, Pallas kernels, finish(): pl.pallas_call(finish_kernel, in_specs=[smem, smem, vmem, vmem, vmem], ou...  21.3 us
    unnamed x9, local copies, waits for them, and re-layouts  5.15 us

profile of v6, /device:TPU:1, one launch (start us, length us, event | category | flops | bytes accessed | tf_op | source)
XLA Modules:
  0.0 192.4 jit_solution(8294106214091757701)
XLA Ops:
  0.6 1.4 copy.8.pat_ref
  2.0 52.4 %gather.1 = (bf16[4,2,256,2048]{3,2,1,0:T(8,128)(2,1)}, bf16[2,256,3584]{2,1,0:T(8,128)(2,1)}, f32[8,4,2,56,128]{4,3,2,1,0:T(8,128)}, f32[8,4,2,4,32,128]{5,4,3,2,1,0:T(8,128)}) custom-call(bf16[256,2048]{1,0:T(8,128)(2,1)} %cot.1, bf16[256,3584]{1,0:T(8,128)(2,1)} %hid.1, f32[56,128]{1,0:T(8,128)} %bitcast.18, f32[32,128]{1,0:T(8,128)} %bitcast.19), custom_call_target="tpu_custom_call" | custom-call | bytes 60000000 | tf_op jit(solution)/shard_map/gather/pallas_call | solution.py:302
  54.4 30.9 %local_step.1 = (bf16[256,3584]{1,0:T(8,128)(2,1)}, f32[4,3584,128]{2,1,0:T(8,128)}, f32[32,128,128]{2,1,0:T(8,128)}) custom-call(s32[1]{0:T(128)} %bitcast.core_ref, s32[28,8]{1,0:T(8,128)} %copy.8.pat_ref, bf16[4,512,2048]{2,1,0:T(8,128)(2,1)} %bitcast.20, bf16[512,3584]{1,0:T(8,128)(2,1)} %bitcast.21, bf16[3584,8,128]{2,1,0:T(8,128)(2,1)} %wgt_ref.1, ...), custom_call_target="tpu_custom_call" | custom-call | flops 6000000000 | bytes 36000000 | tf_op jit(solution)/shard_map/local_step/pallas_call | solution.py:120
  85.3 0.0 copy-start
  85.3 1.6 copy-done
  86.9 0.0 copy-start.1
  86.9 0.0 copy-start.2
  86.9 82.0 %reduce.1 = (f32[8,56,128]{2,1,0:T(8,128)S(1)}, f32[8,4,2,4,32,128]{5,4,3,2,1,0:T(8,128)}) custom-call(f32[4,8,4,112,128]{4,3,2,1,0:T(8,128)} %bitcast.17, f32[8,4,4,32,128]{4,3,2,1,0:T(8,128)S(1)} %bitcast.14), custom_call_target="tpu_custom_call" | custom-call | bytes 100000000 | tf_op jit(solution)/shard_map/reduce/pallas_call | solution.py:581
  168.9 0.0 copy-done.1
  168.9 0.0 copy-done.2
  169.0 0.0 copy-start.3
  169.0 2.2 %copy-done.3 = f32[8,4,2,4,32,128]{5,4,3,2,1,0:T(8,128)S(1)} copy-done((f32[8,4,2,4,32,128]{5,4,3,2,1,0:T(8,128)S(1)}, f32[8,4,2,4,32,128]{5,4,3,2,1,0:T(8,128)}, u32[]{:S(2)}) %copy-start.3) | copy-done | bytes 4194328
  171.1 21.3 %finish.1 = f32[56,8,128]{2,1,0:T(8,128)} custom-call(s32[1]{0:T(128)} %bitcast.7.row_ref, s32[28,8]{1,0:T(8,128)S(1)} %copy-done.1, f32[8,56,128]{2,1,0:T(8,128)S(1)} %get-tuple-element.17.grad_ref, f32[8192,128]{1,0:T(8,128)S(1)} %bitcast.15, f32[8192,128]{1,0:T(8,128)S(1)} %bitcast.16), custom_call_target="tpu_custom_call" | custom-call | flops 5000000000 | bytes 9000000 | tf_op jit(solution)/shard_map/finish/pallas_call | solution.py:706
Async XLA Ops:
  85.3 1.6 copy-start
  86.9 82.0 %copy-start.1 = (s32[28,8]{1,0:T(8,128)S(1)}, s32[28,8]{1,0:T(8,128)}, u32[]{:S(2)}) copy-start(s32[28,8]{1,0:T(8,128)} %copy.8.pat_ref) | copy-start | bytes 2692
  86.9 82.0 %copy-start.2 = (f32[8,4,2,4,32,128]{5,4,3,2,1,0:T(8,128)S(1)}, f32[8,4,2,4,32,128]{5,4,3,2,1,0:T(8,128)}, u32[]{:S(2)}) copy-start(f32[8,4,2,4,32,128]{5,4,3,2,1,0:T(8,128)} %get-tuple-element.18) | copy-start | bytes 12582916
  169.0 2.2 %copy-start.3 = (f32[8,4,2,4,32,128]{5,4,3,2,1,0:T(8,128)S(1)}, f32[8,4,2,4,32,128]{5,4,3,2,1,0:T(8,128)}, u32[]{:S(2)}) copy-start(f32[8,4,2,4,32,128]{5,4,3,2,1,0:T(8,128)} %get-tuple-element.19) | copy-start | bytes 12582916

commit v7 on v6

--- a/solution.py
+++ b/solution.py
@@ -508,6 +508,7 @@
     second.start()
     advance(b_rings[:2])
     second.middle()
+    first.along_y()
     received(a_far[0])
     add_into(xg, [0, None, y1], ya.at[0], nz)
     a_near.append(send(xg.at[0, :, y1], ya.at[4], yp))
@@ -515,18 +516,17 @@
     add_into(xg, [1, None, y3], ya.at[1], nz)
     a_near.append(send(xg.at[1, :, y3], ya.at[5], ym))
     advance(b_rings[2:])
-    first.along_y()
+    first.along_z()
     advance(b_rings[:2])
-    first.along_z()
     second.along_y()
+    first.total()
     advance(b_rings[2:])
-    first.total()
     second.along_z()
+    first.back_y()
     advance(b_rings[:2])
-    first.back_y()
     second.total()
+    first.back_x()
     advance(b_rings[2:])
-    first.back_x()
     second.back_y()
     received(a_near[2], a_near[1])
 

time: 193 us -> 188 us (0.974)
  Pallas kernels: 187 us -> 182 us
    pallas_call x1, Pallas kernels: 82 us -> 77.2 us  [reduce_all(): pl.pallas_call(functools.partial(reduce_kernel, ny, nz, nx), in_specs=[an...]
where the time goes in v7:
time: 188 us
  Pallas kernels  182 us (97%)
  local copies, waits for them, and re-layouts  5.15 us (3%)
    pallas_call x1, Pallas kernels, reduce_all(): pl.pallas_call(functools.partial(reduce_kernel, ny, nz, nx), in_specs=[an...  77.2 us
    pallas_call x1, Pallas kernels, gather(): pl.pallas_call(functools.partial(gather_kernel, ny, nz, nx), in_specs=[an...  52.4 us
    pallas_call x1, Pallas kernels, local_step(): pl.pallas_call(functools.partial(local_kernel, 1.0 / all_tokens), grid_sp...  31.2 us
    pallas_call x1, Pallas kernels, finish(): pl.pallas_call(finish_kernel, in_specs=[smem, smem, vmem, vmem, vmem], ou...  21.3 us
    unnamed x9, local copies, waits for them, and re-layouts  5.15 us

profile of v7, /device:TPU:1, one launch (start us, length us, event | category | flops | bytes accessed | tf_op | source)
XLA Modules:
  0.0 187.9 jit_solution(2298230457440336062)
XLA Ops:
  0.6 1.4 copy.8.pat_ref
  2.0 52.4 %gather.1 = (bf16[4,2,256,2048]{3,2,1,0:T(8,128)(2,1)}, bf16[2,256,3584]{2,1,0:T(8,128)(2,1)}, f32[8,4,2,56,128]{4,3,2,1,0:T(8,128)}, f32[8,4,2,4,32,128]{5,4,3,2,1,0:T(8,128)}) custom-call(bf16[256,2048]{1,0:T(8,128)(2,1)} %cot.1, bf16[256,3584]{1,0:T(8,128)(2,1)} %hid.1, f32[56,128]{1,0:T(8,128)} %bitcast.18, f32[32,128]{1,0:T(8,128)} %bitcast.19), custom_call_target="tpu_custom_call" | custom-call | bytes 60000000 | tf_op jit(solution)/shard_map/gather/pallas_call | solution.py:302
  54.4 31.2 %local_step.1 = (bf16[256,3584]{1,0:T(8,128)(2,1)}, f32[4,3584,128]{2,1,0:T(8,128)}, f32[32,128,128]{2,1,0:T(8,128)}) custom-call(s32[1]{0:T(128)} %bitcast.core_ref, s32[28,8]{1,0:T(8,128)} %copy.8.pat_ref, bf16[4,512,2048]{2,1,0:T(8,128)(2,1)} %bitcast.20, bf16[512,3584]{1,0:T(8,128)(2,1)} %bitcast.21, bf16[3584,8,128]{2,1,0:T(8,128)(2,1)} %wgt_ref.1, ...), custom_call_target="tpu_custom_call" | custom-call | flops 6000000000 | bytes 36000000 | tf_op jit(solution)/shard_map/local_step/pallas_call | solution.py:120
  85.7 0.0 copy-start
  85.7 1.6 copy-done
  87.2 0.0 copy-start.1
  87.2 0.0 copy-start.2
  87.2 77.2 %reduce.1 = (f32[8,56,128]{2,1,0:T(8,128)S(1)}, f32[8,4,2,4,32,128]{5,4,3,2,1,0:T(8,128)}) custom-call(f32[4,8,4,112,128]{4,3,2,1,0:T(8,128)} %bitcast.17, f32[8,4,4,32,128]{4,3,2,1,0:T(8,128)S(1)} %bitcast.14), custom_call_target="tpu_custom_call" | custom-call | bytes 100000000 | tf_op jit(solution)/shard_map/reduce/pallas_call | solution.py:581
  164.4 0.0 copy-done.1
  164.4 0.0 copy-done.2
  164.5 0.0 copy-start.3
  164.5 2.2 %copy-done.3 = f32[8,4,2,4,32,128]{5,4,3,2,1,0:T(8,128)S(1)} copy-done((f32[8,4,2,4,32,128]{5,4,3,2,1,0:T(8,128)S(1)}, f32[8,4,2,4,32,128]{5,4,3,2,1,0:T(8,128)}, u32[]{:S(2)}) %copy-start.3) | copy-done | bytes 4194328
  166.6 21.3 %finish.1 = f32[56,8,128]{2,1,0:T(8,128)} custom-call(s32[1]{0:T(128)} %bitcast.7.row_ref, s32[28,8]{1,0:T(8,128)S(1)} %copy-done.1, f32[8,56,128]{2,1,0:T(8,128)S(1)} %get-tuple-element.17.grad_ref, f32[8192,128]{1,0:T(8,128)S(1)} %bitcast.15, f32[8192,128]{1,0:T(8,128)S(1)} %bitcast.16), custom_call_target="tpu_custom_call" | custom-call | flops 5000000000 | bytes 9000000 | tf_op jit(solution)/shard_map/finish/pallas_call | solution.py:706
Async XLA Ops:
  85.7 1.6 copy-start
  87.2 77.2 %copy-start.1 = (s32[28,8]{1,0:T(8,128)S(1)}, s32[28,8]{1,0:T(8,128)}, u32[]{:S(2)}) copy-start(s32[28,8]{1,0:T(8,128)} %copy.8.pat_ref) | copy-start | bytes 2692
  87.2 77.2 %copy-start.2 = (f32[8,4,2,4,32,128]{5,4,3,2,1,0:T(8,128)S(1)}, f32[8,4,2,4,32,128]{5,4,3,2,1,0:T(8,128)}, u32[]{:S(2)}) copy-start(f32[8,4,2,4,32,128]{5,4,3,2,1,0:T(8,128)} %get-tuple-element.18) | copy-start | bytes 12582916
  164.5 2.2 %copy-start.3 = (f32[8,4,2,4,32,128]{5,4,3,2,1,0:T(8,128)S(1)}, f32[8,4,2,4,32,128]{5,4,3,2,1,0:T(8,128)}, u32[]{:S(2)}) copy-start(f32[8,4,2,4,32,128]{5,4,3,2,1,0:T(8,128)} %get-tuple-element.19) | copy-start | bytes 12582916

commit v8 on v7

--- a/solution.py
+++ b/solution.py
@@ -656,16 +656,30 @@
     return -mul(inverse, half_inv) / (math.sqrt(EPS) * jnp.sqrt(frob))
 
 
-def finish_kernel(row_ref, pat_ref, grad_ref, sketch_ref, comp_ref, out_ref, gram_ref, sel_ref):
+def finish_kernel(
+    row_ref, pat_ref, grad_ref, sketch_hbm, comp_hbm, out_ref, gram_ref, sel_ref, sketch_ref, comp_ref, sems
+):
     slots, rows, blk = grad_ref.shape
-    rank = comp_ref.shape[1]
-    width = comp_ref.shape[0]
-    chunk = 1024
+    width, rank = comp_ref.shape
+    parts = sems.shape[1]
+    chunk = width // parts
+
+    def load(i):
+        at = pl.ds(i * chunk, chunk)
+        return (
+            pltpu.make_async_copy(sketch_hbm.at[at], sketch_ref.at[at], sems.at[0, i]),
+            pltpu.make_async_copy(comp_hbm.at[at], comp_ref.at[at], sems.at[1, i]),
+        )
+
+    loads = [load(i) for i in range(parts)]
+    for pair in loads:
+        for copy in pair:
+            copy.start()
     gram_ref[...] = jnp.zeros_like(gram_ref)
-
-    @pl.loop(0, width // chunk)
-    def _(i):
-        at = pl.ds(pl.multiple_of(i * chunk, chunk), chunk)
+    for i in range(parts):
+        for copy in loads[i]:
+            copy.wait()
+        at = pl.ds(i * chunk, chunk)
         st = jnp.concatenate([sketch_ref[at, :], comp_ref[at, :]], axis=1)
         high, low = split_bf16(st)
         dims = (((0,), (0,)), ((), ()))
@@ -705,14 +719,17 @@
     vmem = pl.BlockSpec(memory_space=pltpu.VMEM)
     return pl.pallas_call(
         finish_kernel,
-        in_specs=[smem, smem, vmem, vmem, vmem],
+        in_specs=[smem, smem, vmem] + [pl.BlockSpec(memory_space=pl.ANY)] * 2,
         out_specs=vmem,
         out_shape=jax.ShapeDtypeStruct((rows, slots, blk), F32),
         scratch_shapes=[
             pltpu.VMEM((2, 2 * rank, 2 * rank), F32),
             pltpu.VMEM((2, slots * blk, 2 * rank), F32),
+            pltpu.VMEM(sketch_t.shape, F32),
+            pltpu.VMEM(comp_t.shape, F32),
+            pltpu.SemaphoreType.DMA((2, 8)),
         ],
-        compiler_params=pltpu.CompilerParams(vmem_limit_bytes=40 * MIB),
+        compiler_params=pltpu.CompilerParams(vmem_limit_bytes=60 * MIB),
         cost_estimate=pl.CostEstimate(flops=5_000_000_000, bytes_accessed=9_000_000, transcendentals=0),
         name="finish",
     )(start_row, pattern, grad, sketch_t, comp_t)

time: 188 us -> 187 us (level)
    unnamed x9 -> x5, local copies, waits for them, and re-layouts: 5.15 us -> 3.62 us
where the time goes in v8:
time: 187 us
  Pallas kernels  183 us (98%)
  local copies, waits for them, and re-layouts  3.62 us (2%)
    pallas_call x1, Pallas kernels, reduce_all(): pl.pallas_call(functools.partial(reduce_kernel, ny, nz, nx), in_specs=[an...  76.9 us
    pallas_call x1, Pallas kernels, gather(): pl.pallas_call(functools.partial(gather_kernel, ny, nz, nx), in_specs=[an...  52.4 us
    pallas_call x1, Pallas kernels, local_step(): pl.pallas_call(functools.partial(local_kernel, 1.0 / all_tokens), grid_sp...  31.2 us
    pallas_call x1, Pallas kernels, finish(): pl.pallas_call(finish_kernel, in_specs=[smem, smem, vmem] + [pl.BlockSpec...  22.2 us

profile of v8, /device:TPU:1, one launch (start us, length us, event | category | flops | bytes accessed | tf_op | source)
XLA Modules:
  0.0 187.1 jit_solution(9048040178331631088)
XLA Ops:
  0.6 1.4 copy.8.pat_ref
  2.0 52.4 %gather.1 = (bf16[4,2,256,2048]{3,2,1,0:T(8,128)(2,1)}, bf16[2,256,3584]{2,1,0:T(8,128)(2,1)}, f32[8,4,2,56,128]{4,3,2,1,0:T(8,128)}, f32[8,4,2,4,32,128]{5,4,3,2,1,0:T(8,128)}) custom-call(bf16[256,2048]{1,0:T(8,128)(2,1)} %cot.1, bf16[256,3584]{1,0:T(8,128)(2,1)} %hid.1, f32[56,128]{1,0:T(8,128)} %bitcast.16, f32[32,128]{1,0:T(8,128)} %bitcast.17), custom_call_target="tpu_custom_call" | custom-call | bytes 60000000 | tf_op jit(solution)/shard_map/gather/pallas_call | solution.py:302
  54.4 31.2 %local_step.1 = (bf16[256,3584]{1,0:T(8,128)(2,1)}, f32[4,3584,128]{2,1,0:T(8,128)}, f32[32,128,128]{2,1,0:T(8,128)}) custom-call(s32[1]{0:T(128)} %bitcast.core_ref, s32[28,8]{1,0:T(8,128)} %copy.8.pat_ref, bf16[4,512,2048]{2,1,0:T(8,128)(2,1)} %bitcast.18, bf16[512,3584]{1,0:T(8,128)(2,1)} %bitcast.21, bf16[3584,8,128]{2,1,0:T(8,128)(2,1)} %wgt_ref.1, ...), custom_call_target="tpu_custom_call" | custom-call | flops 6000000000 | bytes 36000000 | tf_op jit(solution)/shard_map/local_step/pallas_call | solution.py:120
  85.7 0.0 copy-start
  85.7 1.6 copy-done
  87.3 76.9 %reduce.1 = (f32[8,56,128]{2,1,0:T(8,128)S(1)}, f32[8,4,2,4,32,128]{5,4,3,2,1,0:T(8,128)}) custom-call(f32[4,8,4,112,128]{4,3,2,1,0:T(8,128)} %bitcast.15, f32[8,4,4,32,128]{4,3,2,1,0:T(8,128)S(1)} %bitcast.14), custom_call_target="tpu_custom_call" | custom-call | bytes 100000000 | tf_op jit(solution)/shard_map/reduce/pallas_call | solution.py:581
  164.1 0.0 copy-start.1
  164.2 0.7 copy-done.1
  164.8 22.2 %finish.1 = f32[56,8,128]{2,1,0:T(8,128)} custom-call(s32[1]{0:T(128)} %bitcast.7.row_ref, s32[28,8]{1,0:T(8,128)} %copy.8.pat_ref, f32[8,56,128]{2,1,0:T(8,128)} %copy-done.1, f32[8192,128]{1,0:T(8,128)} %bitcast.19, f32[8192,128]{1,0:T(8,128)} %bitcast.20), custom_call_target="tpu_custom_call" | custom-call | flops 5000000000 | bytes 9000000 | tf_op jit(solution)/shard_map/finish/pallas_call | solution.py:720
Async XLA Ops:
  85.7 1.6 copy-start
  164.1 0.7 copy-start.1
